TPU v7x, 128 devices: a whole 4x4x4 slice. The times are simulated.
128 devices in a mesh: row: 16 (over z, y), col: 8 (over x, core).
Axes of the slice: x: 4, y: 4, z: 4, core: 2. Of those that a mesh axis runs over, the one named last changes fastest.
Arguments:
- delta: float32 [512, 8192], P('row', 'col'), may hold values from -4 to 4
- counts: int32 [8, 512, 8192], P(None, 'row', 'col'), may hold values from 0 to 32
- nbar: float32 [8], replicated, may hold values from 0.2 to 1
- bias: float32 [8], replicated, may hold values from 0.05 to 0.15
- owner: int32 [32768, 1], P(('row', 'col')), may hold values from 0 to 127; in each aligned block of 256 rows (0 to 255, 256 to 511, ...) at most 4 rows name the same one
- anchor_x: int32 [32768], P(('row', 'col')), may hold values from 0 to 29
- anchor_y: int32 [32768], P(('row', 'col')), may hold values from 0 to 59
- anchor_z: int32 [32768], P(('row', 'col')), may hold values from 0 to 15
Outputs:
- gradient: float32 [512, 8192], P('row', 'col')
- density: float32 [512, 8192], P('row', 'col')
Inputs may be any that keep to these rules, and one draw needn't show every extreme that they name: Within the blocks of one device no owner is named more than 4 times, a bound that some block reaches.
All inputs are finite; a program needn't handle non-finite values.
Results may differ from a plain program's by a relative error of at most 0.0003.
Values sent between devices are 32-bit elements; how exact they have to be, the bound alone decides.
A program may use at most 192 MiB of HBM per device.

v0:
```python
import math

import jax
import jax.numpy as jnp
from jax import lax
from jax.sharding import PartitionSpec as P

GRID = 512
NZ = 16
BX = 2
BY = 4
BZ = 16


PRECISE = lax.Precision.HIGHEST
SECOND_ORDER = 3.0 / 7.0


def padded_2(block, sides, width):
    for axis, dim in sides:
        count = lax.axis_size(axis)
        forward = [(i, i + 1) for i in range(count - 1)]
        forward.append((count - 1, 0))
        backward = [(target, source) for source, target in forward]
        low = lax.ppermute(
            lax.slice_in_dim(block, block.shape[dim] - width, None, axis=dim), axis, forward
        )
        high = lax.ppermute(lax.slice_in_dim(block, 0, width, axis=dim), axis, backward)
        block = jnp.concatenate([low, block, high], axis=dim)
    return block


def angle_pair(length):
    counter = jnp.arange(length, dtype=jnp.int32)
    phase = counter[:, None] * counter[None, :] % length
    angle = phase.astype(jnp.float32) * (2.0 * math.pi / length)
    return (jnp.cos(angle), jnp.sin(angle))


def complex_table(length, inverse):
    cosine, sine = angle_pair(length)
    if inverse:
        cosine = cosine / length
        sine = -sine / length
    upper = jnp.stack([cosine, sine])
    lower = jnp.stack([-sine, cosine])
    return jnp.stack([upper, lower])


def signed_square(counter, length):
    signed = jnp.where(counter <= (length - 1) // 2, counter, counter - length)
    number = signed.astype(jnp.float32) * (2.0 * math.pi / length)
    return number * number


def build_tables():
    forward = complex_table(GRID, False)
    backward = complex_table(GRID, True)
    layer_y = GRID // lax.axis_size("row")
    wave_y = signed_square(
        lax.axis_index("row") * layer_y + jnp.arange(layer_y, dtype=jnp.int32), GRID
    )
    wave_x = signed_square(jnp.arange(GRID, dtype=jnp.int32), GRID)
    half = NZ // 2
    layer_z = half // lax.axis_size("col")
    counter_z = jnp.arange(NZ, dtype=jnp.int32)
    counter_k = jnp.arange(half, dtype=jnp.int32)
    phase = counter_z[:, None] * counter_k[None, :] % NZ
    angle = phase.astype(jnp.float32) * (2.0 * math.pi / NZ)
    cosine = jnp.cos(angle)
    sine = jnp.sin(angle)
    alternate = (1 - 2 * (counter_z % 2)).astype(jnp.float32)
    lowest = counter_k == 0
    into_imag = jnp.where(lowest[None, :], alternate[:, None] * jnp.ones_like(sine), -sine)
    into_z = jnp.stack([cosine, into_imag])
    out_real = jnp.where(lowest[:, None], jnp.ones_like(cosine.T), 2.0 * cosine.T) / NZ
    out_imag = (
        jnp.where(lowest[:, None], alternate[None, :] * jnp.ones_like(sine.T), -2.0 * sine.T) / NZ
    )
    out_of_z = jnp.stack([out_real, out_imag])
    planes = lax.axis_index("col") * layer_z + jnp.arange(layer_z, dtype=jnp.int32)
    planes = jnp.concatenate([planes, jnp.full((1,), half, jnp.int32)])
    wave_z = signed_square(planes, NZ)
    total = wave_z[:, None, None] + wave_y[None, :, None] + wave_x[None, None, :]
    safe = jnp.where(total > 0, total, jnp.ones_like(total))
    factor = jnp.where(total > 0, -1.0 / safe, jnp.zeros_like(total))
    return (into_z, forward, backward, out_of_z, factor)


def by_half_columns(spectrum):
    return lax.all_to_all(spectrum, "col", split_axis=2, concat_axis=3, tiled=True)


def by_rows(spectrum):
    return lax.all_to_all(spectrum, "row", split_axis=2, concat_axis=3, tiled=True)


def middle(spectrum, forward, backward, factor):
    spectrum = jnp.einsum("cxzy,dcyk->dzkx", spectrum, forward, precision=PRECISE)
    spectrum = by_rows(spectrum)
    spectrum = jnp.einsum("czyx,dcxk->dzyk", spectrum, forward, precision=PRECISE) * factor[None]
    spectrum = jnp.einsum("czyk,dckx->dzxy", spectrum, backward, precision=PRECISE)
    spectrum = by_rows(spectrum)
    return jnp.einsum("czxk,dcky->dxyz", spectrum, backward, precision=PRECISE)


def poisson(source, tables):
    into_z, forward, backward, out_of_z, factor = tables
    spectrum = jnp.einsum("xyz,dzk->dxky", source, into_z, precision=PRECISE)
    spectrum = by_half_columns(spectrum)
    layer = spectrum.shape[2]
    first_col = (lax.axis_index("col") == 0).astype(jnp.float32)
    head = spectrum
    nyquist = jnp.stack([head[1] * first_col, jnp.zeros_like(head[1])])
    head = jnp.stack([head[0], head[1] * (1.0 - first_col)])
    spectrum = jnp.concatenate([head, spectrum[:, :, 1:], nyquist], axis=2)
    spectrum = middle(spectrum, forward, backward, factor)
    top = spectrum[:, :, :, 0:1]
    tail = spectrum[:, :, :, layer : layer + 1]
    top_imag = top[1] * (1.0 - first_col) + tail[0] * first_col
    spectrum = jnp.concatenate([jnp.stack([top[0], top_imag]), spectrum[:, :, :, 1:layer]], axis=3)
    spectrum = by_half_columns(spectrum)
    return jnp.einsum("cxyk,ckz->xyz", spectrum, out_of_z, precision=PRECISE)


def extend(stack):
    return padded_2(stack, (("row", 1), ("col", 2)), 1)


def inner(padded):
    return padded[:, 1:-1, 1:-1]


def slope_x(padded):
    return (padded[:, 2:, 1:-1] - padded[:, :-2, 1:-1]) * 0.5


def slope_y(padded):
    return (padded[:, 1:-1, 2:] - padded[:, 1:-1, :-2]) * 0.5


def slope_z(padded):
    center = inner(padded)
    return (jnp.roll(center, -1, axis=3) - jnp.roll(center, 1, axis=3)) * 0.5


def bend_x(padded):
    return padded[:, 2:, 1:-1] - 2.0 * inner(padded) + padded[:, :-2, 1:-1]


def bend_y(padded):
    return padded[:, 1:-1, 2:] - 2.0 * inner(padded) + padded[:, 1:-1, :-2]


def bend_z(padded):
    center = inner(padded)
    return jnp.roll(center, -1, axis=3) - 2.0 * center + jnp.roll(center, 1, axis=3)


def twist_xy(padded):
    differ = padded[:, 2:, :] - padded[:, :-2, :]
    return (differ[:, :, 2:] - differ[:, :, :-2]) * 0.25


def twist_xz(padded):
    differ = padded[:, 2:, 1:-1] - padded[:, :-2, 1:-1]
    return (jnp.roll(differ, -1, axis=3) - jnp.roll(differ, 1, axis=3)) * 0.25


def twist_yz(padded):
    differ = padded[:, 1:-1, 2:] - padded[:, 1:-1, :-2]
    return (jnp.roll(differ, -1, axis=3) - jnp.roll(differ, 1, axis=3)) * 0.25


def to_blocks(stack):
    parts, size_x, size_y, size_z = stack.shape
    shaped = stack.reshape(parts, size_x // BX, BX, size_y // BY, BY, size_z // BZ, BZ)
    return shaped.transpose(1, 3, 5, 0, 2, 4, 6).reshape(-1, parts, BX * BY * BZ)


def from_blocks(blocks, size_x, size_y):
    parts = blocks.shape[1]
    shaped = blocks.reshape(size_x // BX, size_y // BY, NZ // BZ, parts, BX, BY, BZ)
    return shaped.transpose(3, 0, 4, 1, 5, 2, 6).reshape(parts, size_x, size_y, NZ)


def handover(payload):
    return lax.all_to_all(payload, ("row", "col"), split_axis=0, concat_axis=0, tiled=True)


def particle_steps():
    particle = jnp.arange(BX * BY * BZ, dtype=jnp.int32)
    return (particle // (BY * BZ), particle // BZ % BY, particle % BZ)


def corner_weights(frac, steps, extent):
    offset = jnp.arange(extent + 1, dtype=jnp.int32)
    lower = (offset[None, :] == steps[:, None]).astype(jnp.float32)
    upper = (offset[None, :] == steps[:, None] + 1).astype(jnp.float32)
    weight = (1.0 - frac)[:, :, None] * lower[None] + frac[:, :, None] * upper[None]
    return (weight, upper - lower)


def place_table(anchor, extent, length, wrap):
    offset = jnp.arange(extent + 1, dtype=jnp.int32)
    spot = anchor[:, None] + offset[None, :]
    if wrap:
        spot = spot % length
    return (spot[:, :, None] == jnp.arange(length, dtype=jnp.int32)[None, None, :]).astype(
        jnp.float32
    )


def block_terms(part, width_x, width_y):
    frac, anchors, flag = part
    step_x, step_y, step_z = particle_steps()
    weight_x, change_x = corner_weights(frac[:, 0], step_x, BX)
    weight_y, change_y = corner_weights(frac[:, 1], step_y, BY)
    weight_z, change_z = corner_weights(frac[:, 2], step_z, BZ)
    near_x = place_table(anchors[:, 0], BX, width_x, False)
    near_y = place_table(anchors[:, 1], BY, width_y, False)
    near_z = place_table(anchors[:, 2], BZ, NZ, True)
    return (weight_x, weight_y, weight_z, change_x, change_y, change_z, near_x, near_y, near_z)


def on_device(delta, counts, nbar, bias, owner, anchor_x, anchor_y, anchor_z):
    row_count = lax.axis_size("row")
    col_count = lax.axis_size("col")
    devices = row_count * col_count
    width_x = delta.shape[0]
    width_y = delta.shape[1] // NZ
    block_size = BX * BY * BZ
    tables = build_tables()
    first = poisson(delta.reshape(width_x, width_y, NZ), tables)
    padded = extend(first[None])
    along_xx = bend_x(padded)[0]
    along_yy = bend_y(padded)[0]
    along_zz = bend_z(padded)[0]
    along_xy = twist_xy(padded)[0]
    along_xz = twist_xz(padded)[0]
    along_yz = twist_yz(padded)[0]
    source = (
        along_xx * along_yy
        + along_xx * along_zz
        + along_yy * along_zz
        - along_xy * along_xy
        - along_xz * along_xz
        - along_yz * along_yz
    )
    total = first + SECOND_ORDER * poisson(source, tables)
    padded = extend(total[None])
    shifts = jnp.concatenate([0.5 - slope_x(padded), 0.5 - slope_y(padded), 0.5 - slope_z(padded)])
    moving = to_blocks(shifts)
    block_count = moving.shape[0]
    tags = jnp.stack([anchor_x, anchor_y, anchor_z, jnp.ones_like(anchor_x)], axis=1).astype(
        jnp.float32
    )
    tags = jnp.concatenate([tags, jnp.zeros((block_count, block_size - 4), jnp.float32)], axis=1)
    payload = jnp.concatenate([moving, tags[:, None, :]], axis=1)
    target = owner[:, 0]
    chosen = (target[:, None] == jnp.arange(devices, dtype=jnp.int32)[None, :]).astype(jnp.int32)
    earlier = jnp.cumsum(chosen, axis=0) - chosen
    position = jnp.sum(earlier * chosen, axis=1)
    capacity = max(2, 2 * block_count // devices)
    slot_count = devices * capacity
    slot_index = target * capacity + position
    empty = jnp.zeros((slot_count, 4, block_size), jnp.float32)
    outgoing = empty.at[slot_index].set(payload)
    arrived = handover(outgoing.reshape(devices, capacity, 4, block_size))
    arrived = arrived.reshape(slot_count, 4, block_size)
    group = math.gcd(slot_count, 256)
    turns = slot_count // group
    fractions = arrived[:, 0:3].reshape(turns, group, 3, block_size)
    anchors = arrived[:, 3, 0:3].astype(jnp.int32).reshape(turns, group, 3)
    flags = arrived[:, 3, 3].reshape(turns, group)
    corner_count = (BX + 1) * (BY + 1)

    def paint_group(carry, part):
        weight_x, weight_y, weight_z, change_x, change_y, change_z, near_x, near_y, near_z = (
            block_terms(part, width_x, width_y)
        )
        weight_x = weight_x * part[2][:, None, None]
        pair = (weight_x[:, :, :, None] * weight_y[:, :, None, :]).reshape(
            group, block_size, corner_count
        )
        box = jnp.einsum("spe,spc->sec", pair, weight_z, precision=PRECISE)
        layer = jnp.einsum("sec,scz->sez", box, near_z, precision=PRECISE).reshape(
            group, BX + 1, BY + 1, NZ
        )
        spread = jnp.einsum("sabz,sby->sayz", layer, near_y, precision=PRECISE).reshape(
            group * (BX + 1), width_y * NZ
        )
        placed = jnp.einsum(
            "kx,kc->xc", near_x.reshape(group * (BX + 1), width_x), spread, precision=PRECISE
        )
        return (carry + placed, None)

    density, unused = lax.scan(
        paint_group, jnp.zeros((width_x, width_y * NZ), jnp.float32), (fractions, anchors, flags)
    )
    contrast = density - 1.0
    rate = nbar[:, None, None] * jnp.exp(bias[:, None, None] * contrast[None])
    pull = jnp.sum(bias[:, None, None] * (counts.astype(jnp.float32) - rate), axis=0)

    def pull_group(carry, part):
        weight_x, weight_y, weight_z, change_x, change_y, change_z, near_x, near_y, near_z = (
            block_terms(part, width_x, width_y)
        )
        picked = jnp.einsum(
            "kx,xc->kc", near_x.reshape(group * (BX + 1), width_x), pull, precision=PRECISE
        )
        picked = picked.reshape(group, BX + 1, width_y, NZ)
        picked = jnp.einsum("sayz,sby->sabz", picked, near_y, precision=PRECISE).reshape(
            group, corner_count, NZ
        )
        box = jnp.einsum("sez,scz->sec", picked, near_z, precision=PRECISE)
        along = jnp.einsum("sec,spc->spe", box, weight_z, precision=PRECISE)
        across = jnp.einsum("sec,pc->spe", box, change_z, precision=PRECISE)
        pair = (weight_x[:, :, :, None] * weight_y[:, :, None, :]).reshape(
            group, block_size, corner_count
        )
        tilt_x = (change_x[None, :, :, None] * weight_y[:, :, None, :]).reshape(
            group, block_size, corner_count
        )
        tilt_y = (weight_x[:, :, :, None] * change_y[None, :, None, :]).reshape(
            group, block_size, corner_count
        )
        force_x = jnp.sum(tilt_x * along, axis=2)
        force_y = jnp.sum(tilt_y * along, axis=2)
        force_z = jnp.sum(pair * across, axis=2)
        forces = jnp.stack([force_x, force_y, force_z], axis=1) * part[2][:, None, None]
        return (carry, forces)

    unused, forces = lax.scan(pull_group, jnp.zeros((), jnp.float32), (fractions, anchors, flags))
    returned = handover(forces.reshape(devices, capacity, 3, block_size))
    returned = returned.reshape(slot_count, 3, block_size)[slot_index]
    pulled = from_blocks(returned, width_x, width_y)
    padded = extend(pulled)
    gradient_total = slope_x(padded[0:1])[0] + slope_y(padded[1:2])[0] + slope_z(padded[2:3])[0]
    gradient_source = poisson(SECOND_ORDER * gradient_total, tables)
    weights = jnp.stack(
        [
            gradient_source * (along_yy + along_zz),
            gradient_source * (along_xx + along_zz),
            gradient_source * (along_xx + along_yy),
            -2.0 * gradient_source * along_xy,
            -2.0 * gradient_source * along_xz,
            -2.0 * gradient_source * along_yz,
        ]
    )
    padded = extend(weights)
    gradient_first = (
        gradient_total + bend_x(padded[0:1])[0] + bend_y(padded[1:2])[0] + bend_z(padded[2:3])[0]
    )
    gradient_first = (
        gradient_first
        + twist_xy(padded[3:4])[0]
        + twist_xz(padded[4:5])[0]
        + twist_yz(padded[5:6])[0]
    )
    gradient = poisson(gradient_first, tables)
    return (gradient.reshape(width_x, width_y * NZ), density)


def solution(mesh):
    return jax.shard_map(
        on_device,
        mesh=mesh,
        in_specs=(
            P("row", "col"),
            P(None, "row", "col"),
            P(),
            P(),
            P(("row", "col"), None),
            P(("row", "col")),
            P(("row", "col")),
            P(("row", "col")),
        ),
        out_specs=(P("row", "col"), P("row", "col")),
        check_vma=False,
    )
```

profile of v0, /device:TPU:1, one launch (start us, length us, event | category | flops | bytes accessed | tf_op | source)
XLA Modules:
  0.0 769.3 jit_solution(12748477835814942043)
XLA Ops:
  3.4 5.8 all-to-all-start
  18.0 5.3 broadcast_multiply_fusion.1
  36.1 5.0 fusion.100
  43.8 7.8 %all-to-all-start.1 = ((f32[16,1,4096]{2,1,0:T(1,128)}), f32[16,1,4096]{2,1,0:T(1,128)S(1)}, u32[]{:S(2)}, u32[]{:S(2)}) async-start(f32[16,1,4096]{2,1,0:T(1,128)} %reshape.1902), calls=%async_computation.1 | async-start | bytes 524288 | tf_op jit(solution)/shard_map/all_to_all | solution.py:95
  51.7 8.4 %all-to-all-done.1 = f32[16,1,4096]{2,1,0:T(1,128)S(1)} async-done(((f32[16,1,4096]{2,1,0:T(1,128)}), f32[16,1,4096]{2,1,0:T(1,128)S(1)}, u32[]{:S(2)}, u32[]{:S(2)}) %all-to-all-start.1) | async-done | bytes 262176 | tf_op jit(solution)/shard_map/all_to_all | solution.py:95
  65.4 5.1 fusion.130
  80.7 6.5 all-to-all-done.2
  100.9 6.7 all-to-all-start.3
  107.7 5.2 all-to-all-done.3
  131.9 5.8 all-to-all-start.4
  144.5 5.7 fusion.103
  159.0 6.1 all-to-all-done.5
  172.1 5.1 fusion.124
  188.6 6.9 all-to-all-done.6
  210.9 6.0 all-to-all-start.7
  216.9 5.3 all-to-all-done.7
  253.6 7.0 scatter_fusion
  261.8 7.3 all-to-all-start.8
  269.2 19.2 %all-to-all-done.8 = f32[128,4,4,128]{3,1,2,0:T(4,128)S(1)} async-done(((f32[128,4,4,128]{3,1,2,0:T(4,128)}), f32[128,4,4,128]{3,1,2,0:T(4,128)S(1)}, u32[]{:S(2)}, u32[]{:S(2)}) %all-to-all-start.8) | async-done | bytes 1048608 | tf_op jit(solution)/shard_map/all_to_all | solution.py:188
  290.6 113.2 %while.28 = (s32[]{:T(128)}, f32[32,1024]{1,0:T(8,128)S(1)}, s32[2,256,3]{1,2,0:T(4,128)S(1)}, f32[2,256,3,128]{3,1,2,0:T(8,128)}, f32[2,256]{1,0:T(2,128)}, /*index=5*/s32[]{:T(128)}, s32[]{:T(128)}) while((s32[]{:T(128)}, f32[32,1024]{1,0:T(8,128)S(1)}, s32[2,256,3]{1,2,0:T(4,128)S(1)}, f32[2,256,3,128]{3,1,2,0:T(8,128)}, ...), condition=%wide.region_5.6_spmd.clone, body=%wide.region_4.5_spmd.clone.sunk | while | flops 465442432 | bytes 30441568 | solution.py:298
  293.1 5.9 fusion.474
  303.3 7.3 convolution_bitcast_fusion.19
  310.6 14.5 %copy.819 = f32[256,3,64,16]{3,2,1,0:T(8,128)} copy(f32[256,3,64,16]{2,3,1,0:T(8,128)} %convolution_bitcast_fusion.19) | data formatting | bytes 6291456 | tf_op jit(solution)/shard_map/while/body/eval_jaxpr/sabz,sby->sayz/transpose | solution.py:290
  325.2 20.5 %reshape.1933 = f32[768,1024]{1,0:T(8,128)S(1)} reshape(f32[256,3,64,16]{3,2,1,0:T(8,128)} %copy.819) | data formatting | bytes 6291456 | tf_op jit(solution)/shard_map/while/body/eval_jaxpr/reshape | solution.py:290
  349.6 5.9 fusion.474
  359.8 7.3 convolution_bitcast_fusion.19
  367.1 14.5 %copy.819 = f32[256,3,64,16]{3,2,1,0:T(8,128)} copy(f32[256,3,64,16]{2,3,1,0:T(8,128)} %convolution_bitcast_fusion.19) | data formatting | bytes 6291456 | tf_op jit(solution)/shard_map/while/body/eval_jaxpr/sabz,sby->sayz/transpose | solution.py:290
  381.7 20.5 %reshape.1933 = f32[768,1024]{1,0:T(8,128)S(1)} reshape(f32[256,3,64,16]{3,2,1,0:T(8,128)} %copy.819) | data formatting | bytes 6291456 | tf_op jit(solution)/shard_map/while/body/eval_jaxpr/reshape | solution.py:290
  406.4 116.5 %while.27 = (s32[]{:T(128)}, f32[2,256,3,128]{3,1,0,2:T(8,128)}, f32[2,256,3,128]{3,1,2,0:T(8,128)}, s32[2,256,3]{1,2,0:T(4,128)S(1)}, f32[32,1024]{0,1:T(8,128)}, /*index=5*/f32[2,256]{1,0:T(2,128)}, s32[]{:T(128)}) while((s32[]{:T(128)}, f32[2,256,3,128]{3,1,0,2:T(8,128)}, f32[2,256,3,128]{3,1,2,0:T(8,128)}, s32[2,256,3]{1,2,0:T(4,128)S(1)}, ...), condition=%wide.region_11.12_spmd, body=%wide.region_7.11_spmd.sunk | while | flops 569693440 | bytes 49119436 | solution.py:334
  410.2 5.2 copy.812
  415.4 18.5 %convolution_bitcast_fusion.18 = f32[256,3,5,16]{3,2,1,0:T(8,128)S(1)} fusion(f32[256,3,64,16]{2,3,1,0:T(8,128)} %copy.812, s32[256,5]{1,0:T(8,128)S(1)} %iota_add_fusion.9), kind=kOutput, calls=%fused_computation.18.clone.1 | convolution fusion | flops 47267840 | bytes 3396608 | tf_op jit(solution)/shard_map/while/body/eval_jaxpr/sayz,sby->sabz/dot_general | solution.py:313
  443.9 8.6 %fusion.460 = (f32[256,128]{1,0:T(8,128)S(1)}, f32[256,128]{1,0:T(8,128)S(1)}) fusion(f32[256,128,15]{1,0,2:T(8,128)} %bitcast.836, f32[128,15]{0,1:T(8,128)S(1)} %mul.1934, f32[128,15]{0,1:T(8,128)S(1)} %mul.1936, f32[256,128,15]{1,0,2:T(8,128)} %bitcast.838, f32[256,15,17]{2,1,0:T(8,128)S(1)} %copy-done, f32[128,17]{0,1:T(8,128)S(1)} %fusion.458, ...), kind=kOutput, calls=%fused_computation.11.clone.1 | convolution fusion | flops 104824832 | bytes 4750336 | tf_op jit(solution)/shard_map/while/body/eval_jaxpr/sec,spc->spe/dot_general | solution.py:317
  468.1 5.2 copy.812
  473.4 18.5 %convolution_bitcast_fusion.18 = f32[256,3,5,16]{3,2,1,0:T(8,128)S(1)} fusion(f32[256,3,64,16]{2,3,1,0:T(8,128)} %copy.812, s32[256,5]{1,0:T(8,128)S(1)} %iota_add_fusion.9), kind=kOutput, calls=%fused_computation.18.clone.1 | convolution fusion | flops 47267840 | bytes 3396608 | tf_op jit(solution)/shard_map/while/body/eval_jaxpr/sayz,sby->sabz/dot_general | solution.py:313
  501.9 8.6 %fusion.460 = (f32[256,128]{1,0:T(8,128)S(1)}, f32[256,128]{1,0:T(8,128)S(1)}) fusion(f32[256,128,15]{1,0,2:T(8,128)} %bitcast.836, f32[128,15]{0,1:T(8,128)S(1)} %mul.1934, f32[128,15]{0,1:T(8,128)S(1)} %mul.1936, f32[256,128,15]{1,0,2:T(8,128)} %bitcast.838, f32[256,15,17]{2,1,0:T(8,128)S(1)} %copy-done, f32[128,17]{0,1:T(8,128)S(1)} %fusion.458, ...), kind=kOutput, calls=%fused_computation.11.clone.1 | convolution fusion | flops 104824832 | bytes 4750336 | tf_op jit(solution)/shard_map/while/body/eval_jaxpr/sec,spc->spe/dot_general | solution.py:317
  516.3 4.7 fusion.455
  529.5 16.5 %all-to-all-done.9 = f32[128,4,3,128]{3,1,2,0:T(4,128)S(1)} async-done(((f32[128,4,3,128]{3,1,2,0:T(4,128)}), f32[128,4,3,128]{3,1,2,0:T(4,128)S(1)}, u32[]{:S(2)}, u32[]{:S(2)}) %all-to-all-start.9) | async-done | bytes 786464 | tf_op jit(solution)/shard_map/all_to_all | solution.py:188
  573.7 9.2 %all_to_all.262 = f32[8,1,4096]{2,1,0:T(1,128)S(1)} all-to-all(f32[8,1,4096]{2,1,0:T(1,128)S(1)} %reshape.1916), channel_id=1, replica_groups=mesh['row'=16,'col'=8] {'col'}, dimensions={0} | all-to-all | bytes 262144 | tf_op jit(solution)/shard_map/all_to_all | solution.py:91
  590.6 10.7 %all_to_all.263 = f32[16,1,4096]{2,1,0:T(1,128)S(1)} all-to-all(f32[16,1,4096]{2,1,0:T(1,128)S(1)} %reshape.1918), channel_id=1, replica_groups=mesh['row'=16,'col'=8] {'row'}, dimensions={0} | all-to-all | bytes 524288 | tf_op jit(solution)/shard_map/all_to_all | solution.py:95
  604.5 5.1 fusion.118
  614.2 10.5 %all_to_all.264 = f32[16,1,4096]{2,1,0:T(1,128)S(1)} all-to-all(f32[16,1,4096]{2,1,0:T(1,128)S(1)} %reshape.1920), channel_id=1, replica_groups=mesh['row'=16,'col'=8] {'row'}, dimensions={0} | all-to-all | bytes 524288 | tf_op jit(solution)/shard_map/all_to_all | solution.py:95
  639.7 10.8 %all_to_all.265 = f32[8,1,4096]{2,1,0:T(1,128)S(1)} all-to-all(f32[8,1,4096]{2,1,0:T(1,128)S(1)} %reshape.1922), channel_id=1, replica_groups=mesh['row'=16,'col'=8] {'col'}, dimensions={0} | all-to-all | bytes 262144 | tf_op jit(solution)/shard_map/all_to_all | solution.py:91
  688.1 9.1 %all_to_all.266 = f32[8,1,4096]{2,1,0:T(1,128)S(1)} all-to-all(f32[8,1,4096]{2,1,0:T(1,128)S(1)} %reshape.1924), channel_id=1, replica_groups=mesh['row'=16,'col'=8] {'col'}, dimensions={0} | all-to-all | bytes 262144 | tf_op jit(solution)/shard_map/all_to_all | solution.py:91
  698.7 5.0 fusion.109
  705.4 10.7 %all_to_all.267 = f32[16,1,4096]{2,1,0:T(1,128)S(1)} all-to-all(f32[16,1,4096]{2,1,0:T(1,128)S(1)} %reshape.1926), channel_id=1, replica_groups=mesh['row'=16,'col'=8] {'row'}, dimensions={0} | all-to-all | bytes 524288 | tf_op jit(solution)/shard_map/all_to_all | solution.py:95
  721.4 5.1 fusion.136
  731.1 10.4 %all_to_all.268 = f32[16,1,4096]{2,1,0:T(1,128)S(1)} all-to-all(f32[16,1,4096]{2,1,0:T(1,128)S(1)} %reshape.1928), channel_id=1, replica_groups=mesh['row'=16,'col'=8] {'row'}, dimensions={0} | all-to-all | bytes 524288 | tf_op jit(solution)/shard_map/all_to_all | solution.py:95
  754.5 10.8 %all_to_all.269 = f32[8,1,4096]{2,1,0:T(1,128)S(1)} all-to-all(f32[8,1,4096]{2,1,0:T(1,128)S(1)} %reshape.1930), channel_id=1, replica_groups=mesh['row'=16,'col'=8] {'col'}, dimensions={0} | all-to-all | bytes 262144 | tf_op jit(solution)/shard_map/all_to_all | solution.py:91
  (596 shorter events, 355.2 us)
Async XLA Ops:
  0.6 8.6 %copy-start.72 = (f32[16]{0:T(128)}, f32[16]{0:T(128)S(1)}, u32[]{:S(2)}) copy-start(f32[16]{0:T(128)S(1)} %fusion.333) | copy-start | bytes 196
  0.7 8.5 %copy-start.74 = (pred[8]{0:T(512)(128)(4,1)}, pred[8]{0:T(512)(128)(4,1)S(1)}, u32[]{:S(2)}) copy-start(pred[8]{0:T(512)(128)(4,1)S(1)} %iota_compare_fusion.27) | copy-start | bytes 28
  2.2 128.1 %copy-start.55 = (f32[1,16,8]{1,2,0:T(8,128)}, f32[1,16,8]{1,2,0:T(8,128)S(1)}, u32[]{:S(2)}) copy-start(f32[1,16,8]{1,2,0:T(8,128)S(1)} %get-tuple-element.456) | copy-start | bytes 1540
  2.2 128.1 %copy-start.57 = (f32[1,16,8]{1,2,0:T(8,128)}, f32[1,16,8]{1,2,0:T(8,128)S(1)}, u32[]{:S(2)}) copy-start(f32[1,16,8]{1,2,0:T(8,128)S(1)} %get-tuple-element.457) | copy-start | bytes 1540
  3.4 30.7 %all-to-all-start = ((f32[8,1,4096]{2,1,0:T(1,128)}), f32[8,1,4096]{2,1,0:T(1,128)S(1)}, u32[]{:S(2)}, u32[]{:S(2)}) async-start(f32[8,1,4096]{2,1,0:T(1,128)} %reshape.1900), calls=%async_computation | async-start | bytes 262144 | tf_op jit(solution)/shard_map/all_to_all | solution.py:91
  34.1 168.4 %copy-start.1 = (f32[1,2,512,512]{3,2,1,0:T(8,128)}, f32[1,2,512,512]{3,2,1,0:T(8,128)S(1)}, u32[]{:S(2)}) copy-start(f32[1,2,512,512]{3,2,1,0:T(8,128)S(1)} %get-tuple-element.388) | copy-start | bytes 6291460
  43.8 16.3 %all-to-all-start.1 = ((f32[16,1,4096]{2,1,0:T(1,128)}), f32[16,1,4096]{2,1,0:T(1,128)S(1)}, u32[]{:S(2)}, u32[]{:S(2)}) async-start(f32[16,1,4096]{2,1,0:T(1,128)} %reshape.1902), calls=%async_computation.1 | async-start | bytes 524288 | tf_op jit(solution)/shard_map/all_to_all | solution.py:95
  51.7 120.4 %copy-start.27 = (f32[2,32,512]{2,1,0:T(8,128)}, f32[2,32,512]{2,1,0:T(8,128)S(1)}, u32[]{:S(2)}) copy-start(f32[2,32,512]{2,1,0:T(8,128)S(1)} %fusion.281) | copy-start | bytes 393220
  75.8 11.4 %all-to-all-start.2 = ((f32[16,1,4096]{2,1,0:T(1,128)}), f32[16,1,4096]{2,1,0:T(1,128)S(1)}, u32[]{:S(2)}, u32[]{:S(2)}) async-start(f32[16,1,4096]{2,1,0:T(1,128)} %reshape.1904), calls=%async_computation.2 | async-start | bytes 524288 | tf_op jit(solution)/shard_map/all_to_all | solution.py:95
  96.9 10.7 %copy-start.73 = (f32[16]{0:T(128)S(1)}, f32[16]{0:T(128)}, u32[]{:S(2)}) copy-start(f32[16]{0:T(128)} %copy-done.72) | copy-start | bytes 196
  96.9 10.7 %copy-start.75 = (pred[8]{0:T(512)(128)(4,1)S(1)}, pred[8]{0:T(512)(128)(4,1)}, u32[]{:S(2)}) copy-start(pred[8]{0:T(512)(128)(4,1)} %copy-done.74) | copy-start | bytes 28
  100.9 11.9 %all-to-all-start.3 = ((f32[8,1,4096]{2,1,0:T(1,128)}), f32[8,1,4096]{2,1,0:T(1,128)S(1)}, u32[]{:S(2)}, u32[]{:S(2)}) async-start(f32[8,1,4096]{2,1,0:T(1,128)} %reshape.1906), calls=%async_computation.3 | async-start | bytes 262144 | tf_op jit(solution)/shard_map/all_to_all | solution.py:91
  107.7 116.5 %copy-start.59 = (f32[1,8,16]{2,1,0:T(8,128)}, f32[1,8,16]{2,1,0:T(8,128)S(1)}, u32[]{:S(2)}) copy-start(f32[1,8,16]{2,1,0:T(8,128)S(1)} %get-tuple-element.452) | copy-start | bytes 1540
  107.7 116.5 %copy-start.61 = (f32[1,8,16]{2,1,0:T(8,128)}, f32[1,8,16]{2,1,0:T(8,128)S(1)}, u32[]{:S(2)}) copy-start(f32[1,8,16]{2,1,0:T(8,128)S(1)} %get-tuple-element.453) | copy-start | bytes 1540
  115.4 2.6 collective-permute-start
  116.4 6.0 collective-permute-start.1
  117.2 13.1 %copy-start.16 = (f32[32,64,16]{1,2,0:T(8,128)}, f32[32,64,16]{1,2,0:T(8,128)S(1)}, u32[]{:S(2)}) copy-start(f32[32,64,16]{1,2,0:T(8,128)S(1)} %fusion.217) | copy-start | bytes 393220
  122.5 7.0 collective-permute-start.2
  124.8 4.7 collective-permute-start.3
  131.9 11.1 %all-to-all-start.4 = ((f32[8,1,4096]{2,1,0:T(1,128)}), f32[8,1,4096]{2,1,0:T(1,128)S(1)}, u32[]{:S(2)}, u32[]{:S(2)}) async-start(f32[8,1,4096]{2,1,0:T(1,128)} %reshape.1908), calls=%async_computation.4 | async-start | bytes 262144 | tf_op jit(solution)/shard_map/all_to_all | solution.py:91
  150.2 8.7 %copy-start.69 = (s32[256,1]{0,1:T(1,128)S(1)}, s32[256,1]{0,1:T(1,128)}, u32[]{:S(2)}) copy-start(s32[256,1]{0,1:T(1,128)} %param.16) | copy-start | bytes 3076
  153.5 11.6 %all-to-all-start.5 = ((f32[16,1,4096]{2,1,0:T(1,128)}), f32[16,1,4096]{2,1,0:T(1,128)S(1)}, u32[]{:S(2)}, u32[]{:S(2)}) async-start(f32[16,1,4096]{2,1,0:T(1,128)} %reshape.1910), calls=%async_computation.5 | async-start | bytes 524288 | tf_op jit(solution)/shard_map/all_to_all | solution.py:95
  180.7 7.8 %copy-start.77 = (s32[256]{0:T(256)S(1)}, s32[256]{0:T(256)}, u32[]{:S(2)}) copy-start(s32[256]{0:T(256)} %param.18) | copy-start | bytes 3076
  180.8 7.8 %copy-start.78 = (s32[256]{0:T(256)S(1)}, s32[256]{0:T(256)}, u32[]{:S(2)}) copy-start(s32[256]{0:T(256)} %param.17) | copy-start | bytes 3076
  184.1 11.4 %all-to-all-start.6 = ((f32[16,1,4096]{2,1,0:T(1,128)}), f32[16,1,4096]{2,1,0:T(1,128)S(1)}, u32[]{:S(2)}, u32[]{:S(2)}) async-start(f32[16,1,4096]{2,1,0:T(1,128)} %reshape.1912), calls=%async_computation.6 | async-start | bytes 524288 | tf_op jit(solution)/shard_map/all_to_all | solution.py:95
  210.9 11.3 %all-to-all-start.7 = ((f32[8,1,4096]{2,1,0:T(1,128)}), f32[8,1,4096]{2,1,0:T(1,128)S(1)}, u32[]{:S(2)}, u32[]{:S(2)}) async-start(f32[8,1,4096]{2,1,0:T(1,128)} %reshape.1914), calls=%async_computation.7 | async-start | bytes 262144 | tf_op jit(solution)/shard_map/all_to_all | solution.py:91
  225.2 7.8 %collective-permute-start.4 = (f32[1,1,64,16]{2,3,1,0:T(8,128)}, f32[1,1,64,16]{2,3,1,0:T(8,128)}, u32[]{:S(2)}, u32[]{:S(2)}) collective-permute-start(f32[1,1,64,16]{2,3,1,0:T(8,128)} %get-tuple-element.425), channel_id=1, source_target_pairs={{8,0},{16,8},{24,16},{32,24},{40,32},{48,40},{56,48},{64,56},{72,6... | collective-permute-start | bytes 12296 | tf_op jit(solution)/shard_map/ppermute | solution.py:28
  226.2 6.8 collective-permute-start.5
  234.0 6.7 collective-permute-start.6
  236.0 4.7 collective-permute-start.7
  261.8 26.6 %all-to-all-start.8 = ((f32[128,4,4,128]{3,1,2,0:T(4,128)}), f32[128,4,4,128]{3,1,2,0:T(4,128)S(1)}, u32[]{:S(2)}, u32[]{:S(2)}) async-start(f32[128,4,4,128]{3,1,2,0:T(4,128)} %copy.617), calls=%async_computation.8 | async-start | bytes 2097152 | tf_op jit(solution)/shard_map/all_to_all | solution.py:188
  290.6 113.2 %copy-start.79 = (f32[8]{0:T(128)S(1)}, f32[8]{0:T(128)}, u32[]{:S(2)}) copy-start(f32[8]{0:T(128)} %param.14) | copy-start | bytes 100
  290.6 113.2 %copy-start.80 = (f32[8]{0:T(128)S(1)}, f32[8]{0:T(128)}, u32[]{:S(2)}) copy-start(f32[8]{0:T(128)} %param.15) | copy-start | bytes 100
  525.1 20.9 %all-to-all-start.9 = ((f32[128,4,3,128]{3,1,2,0:T(4,128)}), f32[128,4,3,128]{3,1,2,0:T(4,128)S(1)}, u32[]{:S(2)}, u32[]{:S(2)}) async-start(f32[128,4,3,128]{3,1,2,0:T(4,128)} %copy.626), calls=%async_computation.9 | async-start | bytes 1572864 | tf_op jit(solution)/shard_map/all_to_all | solution.py:188
  556.3 3.1 collective-permute-start.8
  557.1 6.0 collective-permute-start.9
  563.9 7.1 collective-permute-start.10
  566.5 5.1 collective-permute-start.11
  573.1 11.4 %copy-start.7 = (f32[1,2,512,512]{3,2,1,0:T(8,128)S(1)}, f32[1,2,512,512]{3,2,1,0:T(8,128)}, u32[]{:S(2)}) copy-start(f32[1,2,512,512]{3,2,1,0:T(8,128)} %get-tuple-element.390) | copy-start | bytes 6291460
  634.5 19.9 %copy-start.15 = (f32[1,32,64,16]{2,3,1,0:T(8,128)S(1)}, f32[1,32,64,16]{2,3,1,0:T(8,128)}, u32[]{:S(2)}) copy-start(f32[1,32,64,16]{2,3,1,0:T(8,128)} %copy-done.14) | copy-start | bytes 393220
  634.5 19.9 %copy-start.17 = (f32[32,64,16]{1,2,0:T(8,128)S(1)}, f32[32,64,16]{1,2,0:T(8,128)}, u32[]{:S(2)}) copy-start(f32[32,64,16]{1,2,0:T(8,128)} %copy-done.16) | copy-start | bytes 393220
  634.5 19.9 %copy-start.60 = (f32[1,8,16]{2,1,0:T(8,128)S(1)}, f32[1,8,16]{2,1,0:T(8,128)}, u32[]{:S(2)}) copy-start(f32[1,8,16]{2,1,0:T(8,128)} %copy-done.59) | copy-start | bytes 1540
  634.5 19.9 %copy-start.62 = (f32[1,8,16]{2,1,0:T(8,128)S(1)}, f32[1,8,16]{2,1,0:T(8,128)}, u32[]{:S(2)}) copy-start(f32[1,8,16]{2,1,0:T(8,128)} %copy-done.61) | copy-start | bytes 1540
  638.0 16.8 %copy-start.19 = (f32[1,32,64,16]{2,3,1,0:T(8,128)S(1)}, f32[1,32,64,16]{2,3,1,0:T(8,128)}, u32[]{:S(2)}) copy-start(f32[1,32,64,16]{2,3,1,0:T(8,128)} %copy-done.18) | copy-start | bytes 393220
  656.1 3.1 collective-permute-start.12
  657.2 6.4 collective-permute-start.13
  669.5 7.1 collective-permute-start.14
  674.6 4.7 collective-permute-start.15
  (63 other events, 178.0 us)
where the time goes:
time: 782 us; the launch traced here: 769 us
  local copies, waits for them, and re-layouts  261 us (33%)
  matrix products  179 us (23%)
  waiting for transfers between devices  97.9 us (13%)
  blocking collectives  82.3 us (11%)
  other arithmetic  72.5 us (9%)
  starting transfers between devices  71.6 us (9%)
    all_to_all x4, blocking collectives, by_rows(): lax.all_to_all(spectrum, 'row', split_axis=2, concat_axis=3, tiled=True)  42.4 us
    unnamed x193, local copies, waits for them, and re-layouts  41.5 us
    reshape x2, local copies, waits for them, and re-layouts, paint_group(): jnp.einsum('sabz,sby->sayz', layer, near_y, precision=PRECISE)  40.9 us
    all_to_all x4, blocking collectives, by_half_columns(): lax.all_to_all(spectrum, 'col', split_axis=2, concat_axis=3, tiled=True)  39.9 us
    dot_general x2, matrix products, pull_group(): jnp.einsum('sayz,sby->sabz', picked, near_y, precision=PRECISE)  36.9 us
    all_to_all x2, waiting for transfers between devices, handover(): lax.all_to_all(payload, ('row', 'col'), split_axis=0, concat_axis=0, tile...  35.7 us
    transpose x2, local copies, waits for them, and re-layouts, paint_group(): jnp.einsum('sabz,sby->sayz', layer, near_y, precision=PRECISE)  29 us
    all_to_all x4, waiting for transfers between devices, by_rows(): lax.all_to_all(spectrum, 'row', split_axis=2, concat_axis=3, tiled=True)  27.9 us
  transfers between devices with their start and end apart: 26, of which 15 were waited for; matrix products, arithmetic and copies ran while one was open for 7% of the time, Pallas kernels for 0%

commit v1 on v0

v1 whole, which is shorter than its diff:
```python
import functools
import math

import jax
import jax.numpy as jnp
import numpy as np
from jax import lax
from jax.experimental import pallas as pl
from jax.experimental.pallas import tpu as pltpu
from jax.sharding import PartitionSpec as P

GRID, NZ = 512, 16
NROW, NCOL = 16, 8
CX, CY = 32, 64
NBIN = 8
XH = 40
SECOND_ORDER = 3.0 / 7.0
F32, BF16 = jnp.float32, jnp.bfloat16
MESH = pl.DeviceIdType.MESH


def real_basis(n):
    k = np.arange(n)
    rows = []
    for m in range(n):
        if m == 0:
            rows.append(np.full(n, 1.0 / math.sqrt(n)))
        elif m < n // 2:
            rows.append(math.sqrt(2.0 / n) * np.cos(2 * np.pi * (m * k % n) / n))
        elif m == n // 2:
            rows.append((1.0 - 2.0 * (k % 2)) / math.sqrt(n))
        else:
            rows.append(math.sqrt(2.0 / n) * np.sin(2 * np.pi * ((m - n // 2) * k % n) / n))
    return np.stack(rows)


def two_terms(table):
    table = table.astype(np.float32)
    high = table.astype(jnp.bfloat16)
    low = (table - high.astype(np.float32)).astype(jnp.bfloat16)
    return high, low


def make_tables():
    basis = real_basis(GRID)
    r, i = np.divmod(np.arange(256), 16)
    first, second = 32 * r + i, 32 * r + 16 + i
    c, k = np.divmod(np.arange(256), 32)
    low, high = 64 * c + k, 64 * c + 32 + k
    fx = np.concatenate(
        [
            basis[low][:, first],
            basis[high][:, second],
            basis[high][:, first],
            basis[low][:, second],
        ]
    )
    fy = basis.T
    gy = np.zeros((GRID, NCOL, 128))
    for c in range(NCOL):
        gy[:, c, :68] = basis[:, (CY * c - 2 + np.arange(68)) % GRID]
    gx = np.zeros((NROW, XH, GRID))
    for r in range(NROW):
        gx[r, :36] = basis[:, (CX * r - 2 + np.arange(36)) % GRID].T
    tables = []
    for t in (fx, fy, gy.reshape(GRID, NCOL * 128), gx.reshape(NROW * XH, GRID)):
        tables.extend(two_terms(t))
    return tables


ZB = real_basis(NZ)


def box_lane(a, b, z):
    if a == 0:
        return b * 16 + z
    if a == 2:
        return 128 + b * 16 + z
    return 80 + b * 16 + z if b < 3 else 208 + (b - 3) * 16 + z


def make_spread():
    e = np.zeros((4, 128, 256), np.float32)
    for dx in range(2):
        for dy in range(2):
            for v in range(4):
                for u in range(2):
                    for z in range(16):
                        e[dx * 2 + dy, 32 * v + 16 * u + z, box_lane(u + dx, v + dy, z)] = 1.0
    return e.reshape(512, 256)


def dot(a, b):
    return lax.dot_general(a, b, (((1,), (0,)), ((), ())), preferred_element_type=F32)


def split(x):
    high = x.astype(BF16)
    return high, (x - high.astype(F32)).astype(BF16)


def split_3(x):
    high = x.astype(BF16)
    rest = x - high.astype(F32)
    middle = rest.astype(BF16)
    return high, middle, (rest - middle.astype(F32)).astype(BF16)


def left_product(high, low, b):
    n = b.shape[1]
    b0, b1, b2 = split_3(b)
    pair = jnp.concatenate([b0, b1], axis=1)
    t = dot(high, pair)
    s = dot(low, pair)
    return t[:, :n] + ((t[:, n:] + s[:, :n]) + (s[:, n:] + dot(high, b2)))


def right_product(a, high, low):
    m = a.shape[0]
    a0, a1, a2 = split_3(a)
    pair = jnp.concatenate([a0, a1], axis=0)
    t = dot(jnp.concatenate([pair, a2], axis=0), high)
    s = dot(pair, low)
    return t[:m] + ((t[m : 2 * m] + s[:m]) + (s[m:] + t[2 * m :]))


def exact_left(zero_one, b):
    n = b.shape[1]
    t = dot(zero_one, jnp.concatenate(split(b), axis=1))
    return t[:, :n] + t[:, n:]


def exact_right(a, zero_one):
    m = a.shape[0]
    t = dot(jnp.concatenate(split(a), axis=0), zero_one)
    return t[:m] + t[m:]


def lanes(shape, axis=1):
    return lax.broadcasted_iota(jnp.int32, shape, axis)


def roll(x, shift, axis):
    shift = shift % x.shape[axis]
    return x if shift == 0 else pltpu.roll(x, shift, axis)


def up(x, axis):
    return roll(x, -1, axis)


def down(x, axis):
    return roll(x, 1, axis)


def forward_z(v):
    even = [v[0]] + [v[z] + v[16 - z] for z in range(1, 8)] + [v[8]]
    odd = [None] + [v[z] - v[16 - z] for z in range(1, 8)]
    out = []
    for m in range(9):
        s = even[0] * float(ZB[m, 0])
        for z in range(1, 9):
            s = s + even[z] * float(ZB[m, z])
        out.append(s)
    for m in range(9, 16):
        s = odd[1] * float(ZB[m, 1])
        for z in range(2, 8):
            s = s + odd[z] * float(ZB[m, z])
        out.append(s)
    return out


def inverse_z(v):
    out = [None] * 16
    for z in range(9):
        even = v[0] * float(ZB[0, z])
        for m in range(1, 9):
            even = even + v[m] * float(ZB[m, z])
        if z in (0, 8):
            out[z] = even
            continue
        odd = v[9] * float(ZB[9, z])
        for m in range(10, 16):
            odd = odd + v[m] * float(ZB[m, z])
        out[z] = even + odd
        out[16 - z] = even - odd
    return out


def exchange(n, me, axis, src, dst, send, recv, own):
    sends, recvs = [], []
    for k in range(1, n):
        peer = lax.rem(me + k, n)
        origin = lax.rem(me + n - k, n)
        copy = pltpu.make_async_remote_copy(
            src_ref=src.at[peer],
            dst_ref=dst.at[me],
            send_sem=send.at[k],
            recv_sem=recv.at[k],
            device_id={axis: peer},
            device_id_type=MESH,
        )
        copy.start()
        sends.append(copy)
        recvs.append(
            pltpu.make_async_remote_copy(
                src_ref=src.at[peer],
                dst_ref=dst.at[origin],
                send_sem=send.at[k],
                recv_sem=recv.at[k],
                device_id={axis: peer},
                device_id_type=MESH,
            )
        )
    copy = pltpu.make_async_copy(src.at[me], dst.at[me], own)
    copy.start()
    return sends, recvs, copy


def arrive(state):
    state[2].wait()
    for copy in state[1]:
        copy.wait_recv()


def poisson_kernel(
    src, *refs
):
    tables = refs[:8]
    out = refs[8]
    mo, r1, pk, r2, zb, r3, xb, r4 = refs[9:17]
    held = refs[17:25]
    tsem, s1, q1, s2, q2, s3, q3, s4, q4, own = refs[25:]
    row, col = lax.axis_index("row"), lax.axis_index("col")

    barrier = pltpu.get_barrier_semaphore()
    for k in range(1, NROW):
        pl.semaphore_signal(
            barrier, inc=1, device_id={"row": lax.rem(row + k, NROW)}, device_id_type=MESH
        )
    for k in range(1, NCOL):
        pl.semaphore_signal(
            barrier, inc=1, device_id={"col": lax.rem(col + k, NCOL)}, device_id_type=MESH
        )
    loads = [
        pltpu.make_async_copy(t, h, tsem.at[i]) for i, (t, h) in enumerate(zip(tables, held))
    ]
    for load in loads:
        load.start()
    for s in range(2):
        rows = pl.ds(8 * s, 8)
        for m, value in enumerate(forward_z([src[z, rows, :] for z in range(16)])):
            mo[m, rows, :] = value
    pl.semaphore_wait(barrier, NROW + NCOL - 2)

    low_half = lanes((256, 128)) < 64
    state1 = exchange(NROW, row, "row", mo, r1, s1, q1, own.at[0])
    for load in loads:
        load.wait()
    fxh, fxl, fyh, fyl, gyh, gyl, gxh, gxl = held

    kx = lanes((64, GRID), 0) + col * 64
    ky = lanes((64, GRID), 1)
    kx = jnp.where(kx <= GRID // 2, kx, kx - GRID // 2).astype(F32) * (2.0 * math.pi / GRID)
    ky = jnp.where(ky <= GRID // 2, ky, ky - GRID // 2).astype(F32) * (2.0 * math.pi / GRID)
    kz = jnp.where(row <= NZ // 2, row, row - NZ // 2)
    kz = jnp.full((64, GRID), kz, jnp.int32).astype(F32) * (2.0 * math.pi / NZ)
    square = kx * kx + ky * ky + kz * kz
    factor = jnp.where(square > 0, -1.0 / jnp.where(square > 0, square, 1.0), 0.0)

    arrive(state1)
    t = left_product(fxh[...], fxl[...], r1[...].reshape(256, 128))
    packed = jnp.where(low_half, t[:256], t[256:512]) + roll(
        jnp.where(low_half, t[512:768], t[768:]), 64, 1
    )
    pk[...] = packed.reshape(NCOL, 32, 128)
    state2 = exchange(NCOL, col, "col", pk, r2, s2, q2, own.at[1])
    arrive(state2)
    half = lanes((32, 128)) < 64
    top, bottom = [], []
    for p in range(4):
        a, b = r2[2 * p], r2[2 * p + 1]
        top.append(jnp.where(half, a, roll(b, 64, 1)))
        bottom.append(jnp.where(half, roll(a, 64, 1), b))
    full = jnp.concatenate(
        [jnp.concatenate(top, axis=1), jnp.concatenate(bottom, axis=1)], axis=0
    )
    modes = right_product(full, fyh[...], fyl[...]) * factor
    back = right_product(modes, gyh[...], gyl[...])
    for c in range(NCOL):
        zb[c] = back[:, 128 * c : 128 * (c + 1)]
    state3 = exchange(NCOL, col, "col", zb, r3, s3, q3, own.at[2])
    arrive(state3)
    xb[...] = left_product(gxh[...], gxl[...], r3[...].reshape(GRID, 128)).reshape(NROW, XH, 128)
    state4 = exchange(NROW, row, "row", xb, r4, s4, q4, own.at[3])
    arrive(state4)
    for s in range(5):
        rows = pl.ds(8 * s, 8)
        for z, value in enumerate(inverse_z([r4[m, rows, :] for m in range(16)])):
            out[z, rows, :] = value
    for state in (state1, state2, state3, state4):
        for copy in state[0]:
            copy.wait_send()


VM = pl.BlockSpec(memory_space=pltpu.VMEM)
ANY = pl.BlockSpec(memory_space=pl.ANY)


def poisson(src, tables):
    buffers = [(NROW, 16, 128), (NCOL, 32, 128), (NCOL, 64, 128), (NROW, XH, 128)]
    scratch = []
    for shape in buffers:
        scratch += [pltpu.VMEM(shape, F32), pltpu.VMEM(shape, F32)]
    scratch += [pltpu.VMEM(t.shape, BF16) for t in tables]
    scratch += [pltpu.SemaphoreType.DMA((8,))]
    for n in (NROW, NCOL, NCOL, NROW):
        scratch += [pltpu.SemaphoreType.DMA((n,)), pltpu.SemaphoreType.DMA((n,))]
    scratch += [pltpu.SemaphoreType.DMA((4,))]
    return pl.pallas_call(
        poisson_kernel,
        out_shape=jax.ShapeDtypeStruct((NZ, XH, 128), F32),
        in_specs=[VM] + [ANY] * 8,
        out_specs=VM,
        scratch_shapes=scratch,
        compiler_params=pltpu.CompilerParams(
            collective_id=0, has_side_effects=True, vmem_limit_bytes=40 << 20
        ),
        name="poisson",
    )(src, *tables)


def pack(f):
    f = roll(f, -2, 0)
    low = roll(f[0:16], -2, 1)
    high = roll(f[16:32], 62, 1)
    return jnp.where(lanes((16, 128)) < 64, low, high)


def curvatures(below, here, above):
    xx = up(here, 0) - 2.0 * here + down(here, 0)
    yy = up(here, 1) - 2.0 * here + down(here, 1)
    zz = above - 2.0 * here + below
    dx = up(here, 0) - down(here, 0)
    dz = above - below
    xy = (up(dx, 1) - down(dx, 1)) * 0.25
    xz = (up(dz, 0) - down(dz, 0)) * 0.25
    yz = (up(dz, 1) - down(dz, 1)) * 0.25
    return xx, yy, zz, xy, xz, yz


def source_kernel(first, out):
    @pl.loop(0, NZ)
    def _(z):
        xx, yy, zz, xy, xz, yz = curvatures(
            first[(z + 15) % 16], first[z], first[(z + 1) % 16]
        )
        out[z] = pack(xx * yy + xx * zz + yy * zz - xy * xy - xz * xz - yz * yz)


def group_roll(x, s):
    z = lanes(x.shape) % 16
    return jnp.where(z >= s, roll(x, s, 1), roll(x, s - 16, 1))


def barrel(x, amount):
    for bit in (1, 2, 4, 8):
        x = jnp.where((amount & bit) > 0, group_roll(x, bit), x)
    return x


def barrel_16(x, amount):
    for bit in (1, 2, 4):
        x = jnp.where((amount & bit) > 0, roll(x, 16 * bit, 1), x)
    return x


def slots(owner_row, owner_col):
    device = lanes((128, 256), 0)
    chosen_t = jnp.where(device == owner_row, 1.0, 0.0)
    order = jnp.where(lanes((256, 256), 0) < lanes((256, 256), 1), 1.0, 0.0)
    earlier_t = dot(chosen_t.astype(BF16), order.astype(BF16))
    along = jnp.sum(earlier_t * chosen_t, axis=0, keepdims=True)
    along = owner_row * 8 + along.astype(jnp.int32)
    chosen = jnp.where(lanes((256, 128)) == owner_col, 1.0, 0.0)
    order = jnp.where(lanes((256, 256), 0) > lanes((256, 256), 1), 1.0, 0.0)
    earlier = dot(order.astype(BF16), chosen.astype(BF16))
    down_ = jnp.sum(earlier * chosen, axis=1, keepdims=True)
    down_ = owner_col * 8 + down_.astype(jnp.int32)
    return along, down_


def paint_kernel(first, second, owner_row, owner_col, ax, ay, az, spread, out, fracs, tz, tt):
    zrows = [None, None, None]
    piece = lanes((16, 128)) // 32
    for axis in range(3):

        @pl.loop(0, NZ)
        def _(z, axis=axis):
            def total(k):
                return first[k] + SECOND_ORDER * second[k]

            if axis == 2:
                slope = total((z + 1) % 16) - total((z + 15) % 16)
            else:
                here = total(z)
                slope = up(here, axis) - down(here, axis)
            value = 0.5 - 0.5 * slope
            value = roll(roll(value, -2, 0)[0:32], -2, 1)
            tz[pl.ds(z, 32, stride=16), :] = value

        for q in range(4):
            tt[q] = jnp.transpose(tz[pl.ds(128 * q, 128), :])[0:64]
        for q in range(4):
            quarter = [tt[q, pl.ds(v, 16, stride=4), :] for v in range(4)]
            for k in range(4):
                block = roll(quarter[0], -32 * k, 1)
                for v in range(1, 4):
                    block = jnp.where(piece == v, roll(quarter[v], 32 * (v - k), 1), block)
                fracs[axis, pl.ds(16 * (4 * q + k), 16), :] = block
    amount = az[...]
    for axis in range(3):
        fracs[axis] = barrel(fracs[axis], amount)
    fx, fy, fz = fracs[0], fracs[1], fracs[2]
    fields = []
    for wx in (1.0 - fx, fx):
        for wy in (1.0 - fy, fy):
            q = wx * wy
            upper = q * fz
            fields.append(q - upper + group_roll(upper, 1))
    box = exact_right(jnp.concatenate(fields, axis=1), spread[...])
    lane = lanes((256, 256))
    box = jnp.where(lane == 240, ax[...].astype(F32), box)
    box = jnp.where(lane == 241, ay[...].astype(F32), box)
    along, _ = slots(owner_row[...], owner_col[...])
    target = jnp.concatenate([along, along + 4], axis=1)
    table = jnp.where(lanes((1024, 512), 0) == target, 1.0, 0.0).astype(BF16)
    stacked = jnp.concatenate([box[:, :128], box[:, 128:]], axis=0)
    out[...] = exact_left(table, stacked)


def owner_kernel(nbar, bias, arrived, counts, density, back, dens, pulls):
    data = arrived[...]
    second = lanes((1024, 128), 0) // 4 % 2
    is_second = second == 1

    def both(lane):
        column = jnp.broadcast_to(data[:, lane : lane + 1], (1024, 128))
        return jnp.where(is_second, column, roll(column, -4, 0)).astype(jnp.int32)

    ax, ay = both(112), both(113)
    flipped = jnp.concatenate(
        [jnp.transpose(data[128 * i : 128 * (i + 1)]) for i in range(8)], axis=1
    )
    second_row = lanes((1, 1024)) // 4 % 2

    def both_row(lane):
        line = flipped[lane : lane + 1]
        line = jnp.where(second_row == 1, line, roll(line, -4, 1))
        return line.astype(jnp.int32)

    ax_row, ay_row = both_row(112), both_row(113)
    base_row = (ay_row >> 3) * 32 + ax_row
    base = (ay >> 3) * 32 + ax
    lane = lanes((1024, 128))
    step = ay & 7
    side_step = (3 * second + 3 + ay) & 7
    stay = lane >= step * 16
    main = barrel_16(jnp.where(lane < 80, data, 0.0), step)
    side_mask = (lane >= 80) & (lane < 112 + 16 * (1 - second))
    side = barrel_16(jnp.where(side_mask, data, 0.0), side_step)
    total = None
    for part, offset in ((main, 2 * second_row), (side, 1)):
        table = jnp.where(lanes((256, 1024), 0) == base_row + offset, 1.0, 0.0).astype(BF16)
        near = split(jnp.where(stay, part, 0.0))
        far = split(jnp.where(stay, 0.0, part))
        t = dot(table, jnp.concatenate([*near, *far], axis=1))
        total = t if total is None else total + t
    near = total[:, :128] + total[:, 128:256]
    far = total[:, 256:384] + total[:, 384:]
    dens[...] = near + jnp.where(lanes((256, 128), 0) >= 32, roll(far, 32, 0), 0.0)
    for j in range(8):
        here = dens[pl.ds(32 * j, 32), :]
        density[:, pl.ds(128 * j, 128)] = here
        contrast = here - 1.0
        pull = jnp.zeros((32, 128), F32)
        for b in range(NBIN):
            rate = nbar[b] * jnp.exp(bias[b] * contrast)
            number = counts[b, :, pl.ds(128 * j, 128)].astype(F32)
            pull = pull + bias[b] * (number - rate)
        pulls[pl.ds(32 * j, 32), :] = pull
    pull = pulls[...]
    ahead = jnp.where(lanes((256, 128), 0) < 224, roll(pull, -32, 0), 0.0)
    both_pulls = jnp.concatenate([*split(pull), *split(ahead)], axis=1)

    def picked(offset, amount):
        wide = jnp.concatenate([base + offset, base + offset], axis=1)
        table = jnp.where(lanes((1024, 256)) == wide, 1.0, 0.0).astype(BF16)
        t = dot(table, both_pulls)
        value = jnp.where(stay, t[:, :128] + t[:, 128:256], t[:, 256:384] + t[:, 384:])
        return barrel_16(value, (8 - amount) & 7)

    back[...] = jnp.where(lane < 80, picked(2 * second, step), picked(1, side_step))


def force_kernel(returned, owner_row, owner_col, az, spread_t, fracs, fx_out, fy_out, fz_out):
    _, place = slots(owner_row[...], owner_col[...])
    target = jnp.concatenate([place, place + 4], axis=0)
    table = jnp.where(lanes((512, 1024)) == target, 1.0, 0.0).astype(BF16)
    t = exact_left(table, returned[...])
    box = jnp.concatenate([t[:256], t[256:]], axis=1)
    corner = exact_right(box, spread_t[...])
    fx, fy, fz = fracs[0], fracs[1], fracs[2]
    along, across = [], []
    for d in range(4):
        here = corner[:, 128 * d : 128 * (d + 1)]
        change = group_roll(here, 15) - here
        along.append(here + fz * change)
        across.append(change)
    amount = (16 - az[...]) & 15
    force_x = (1.0 - fy) * (along[2] - along[0]) + fy * (along[3] - along[1])
    force_y = (1.0 - fx) * (along[1] - along[0]) + fx * (along[3] - along[2])
    force_z = (1.0 - fx) * ((1.0 - fy) * across[0] + fy * across[1]) + fx * (
        (1.0 - fy) * across[2] + fy * across[3]
    )
    piece = lanes((16, 128)) // 32
    for force, out in ((force_x, fx_out), (force_y, fy_out), (force_z, fz_out)):
        force = barrel(force, amount)
        for q in range(4):
            group = [force[16 * (4 * q + k) : 16 * (4 * q + k) + 16] for k in range(4)]
            for v in range(4):
                value = roll(group[0], -32 * v, 1)
                for k in range(1, 4):
                    value = jnp.where(piece == k, roll(group[k], 32 * (k - v), 1), value)
                out[q, pl.ds(v, 16, stride=4), :] = value


def divergence_kernel(fx, fy, fz, x_low, x_high, y_low, y_high, out, tz):
    def wide(ref):
        return jnp.concatenate([ref[q] for q in range(4)], axis=1)

    f = wide(fx)
    lane = lanes((64, 512))
    before = jnp.where(lane < 16, x_low[...], roll(f, 16, 1))
    after = jnp.where(lane >= 496, x_high[...], roll(f, -16, 1))
    total = after - before
    g = wide(fy)
    line = lanes((64, 512), 0)
    before = jnp.where(line == 0, wide(y_low), roll(g, 1, 0))
    after = jnp.where(line == 63, wide(y_high), roll(g, -1, 0))
    total = total + (after - before)
    h = wide(fz)
    z = lane % 16
    after = jnp.where(z == 15, roll(h, 15, 1), roll(h, -1, 1))
    before = jnp.where(z == 0, roll(h, -15, 1), roll(h, 1, 1))
    total = (total + (after - before)) * (0.5 * SECOND_ORDER)
    total = jnp.concatenate([total, jnp.zeros_like(total)], axis=0)
    for q in range(4):
        tz[pl.ds(128 * q, 128), :] = jnp.transpose(total[:, 128 * q : 128 * (q + 1)])
    for z in range(NZ):
        value = tz[pl.ds(z, 32, stride=16), :]
        out[z] = jnp.where(
            lanes((16, 128)) < 64, value[0:16], roll(value[16:32], 64, 1)
        )


def weight_kernel(first, pulled, out, part, wzz, wxz, wyz):
    @pl.loop(0, NZ)
    def _(z):
        xx, yy, zz, xy, xz, yz = curvatures(
            first[(z + 15) % 16], first[z], first[(z + 1) % 16]
        )
        g = pulled[z]
        wx, wy = g * (yy + zz), g * (xx + zz)
        wxy = -2.0 * g * xy
        diff = up(wxy, 0) - down(wxy, 0)
        part[z] = (
            (up(wx, 0) - 2.0 * wx + down(wx, 0))
            + (up(wy, 1) - 2.0 * wy + down(wy, 1))
            + (up(diff, 1) - down(diff, 1)) * 0.25
        )
        wzz[z] = g * (xx + yy)
        wxz[z] = -2.0 * g * xz
        wyz[z] = -2.0 * g * yz

    @pl.loop(0, NZ)
    def _(z):
        a, b = (z + 1) % 16, (z + 15) % 16
        dx, dy = wxz[a] - wxz[b], wyz[a] - wyz[b]
        out[z] = pack(
            part[z]
            + (wzz[a] - 2.0 * wzz[z] + wzz[b])
            + (up(dx, 0) - down(dx, 0)) * 0.25
            + (up(dy, 1) - down(dy, 1)) * 0.25
        )


def local(kernel, outs, scratch=(), smem=0, n=0, name=None):
    many = isinstance(outs, (list, tuple))
    return pl.pallas_call(
        kernel,
        out_shape=outs,
        in_specs=[pl.BlockSpec(memory_space=pltpu.SMEM)] * smem + [VM] * (n - smem),
        out_specs=[VM] * len(outs) if many else VM,
        scratch_shapes=list(scratch),
        compiler_params=pltpu.CompilerParams(vmem_limit_bytes=40 << 20),
        name=name,
    )


def shape(*s):
    return jax.ShapeDtypeStruct(s, F32)


TABLES = make_tables()
SPREAD = make_spread()


def handover(payload):
    moved = lax.all_to_all(
        payload.reshape(128, 8, 128), ("row", "col"), split_axis=0, concat_axis=0, tiled=True
    )
    return moved.reshape(1024, 128)


def neighbours(low, high, axis, count):
    forward = [(i, (i + 1) % count) for i in range(count)]
    backward = [((i + 1) % count, i) for i in range(count)]
    return lax.ppermute(high, axis, forward), lax.ppermute(low, axis, backward)


def on_device(delta, counts, nbar, bias, owner, anchor_x, anchor_y, anchor_z):
    tables = [jnp.asarray(t) for t in TABLES]
    spread = jnp.asarray(SPREAD, BF16)
    spread_t = jnp.asarray(SPREAD.T, BF16)
    owner_row, owner_col = owner.reshape(1, 256), owner
    ax, ay, az = (a.reshape(256, 1) for a in (anchor_x, anchor_y, anchor_z))

    src = delta.reshape(2, 16, CY, NZ).transpose(3, 1, 0, 2).reshape(NZ, 16, 128)
    first = poisson(src, tables)
    src = local(source_kernel, shape(NZ, 16, 128), n=1, name="source")(first)
    second = poisson(src, tables)
    payload, fracs = local(
        paint_kernel,
        [shape(1024, 128), shape(3, 256, 128)],
        [pltpu.VMEM((512, 128), F32), pltpu.VMEM((4, 64, 128), F32)],
        n=8,
        name="paint",
    )(first, second, owner_row, owner_col, ax, ay, az, spread)
    arrived = handover(payload)
    density, back = local(
        owner_kernel,
        [shape(CX, CY * NZ), shape(1024, 128)],
        [pltpu.VMEM((256, 128), F32), pltpu.VMEM((256, 128), F32)],
        smem=2,
        n=4,
        name="owner",
    )(nbar, bias, arrived, counts)
    returned = handover(back)
    fx, fy, fz = local(force_kernel, [shape(4, CY, 128)] * 3, n=6, name="force")(
        returned, owner_row, owner_col, az, spread_t, fracs
    )
    x_low, x_high = neighbours(fx[0, :, :16], fx[3, :, 112:], "row", NROW)
    y_low, y_high = neighbours(fy[:, :1], fy[:, 63:], "col", NCOL)
    x_low = jnp.pad(x_low, ((0, 0), (0, 496)))
    x_high = jnp.pad(x_high, ((0, 0), (496, 0)))
    src = local(
        divergence_kernel,
        shape(NZ, 16, 128),
        [pltpu.VMEM((512, 128), F32)],
        n=7,
        name="divergence",
    )(fx, fy, fz, x_low, x_high, y_low, y_high)
    pulled = poisson(src, tables)
    src = local(
        weight_kernel,
        shape(NZ, 16, 128),
        [pltpu.VMEM((NZ, XH, 128), F32)] * 4,
        n=2,
        name="weights",
    )(first, pulled)
    last = poisson(src, tables)
    gradient = pulled[:, 2:34, 2:66] * (1.0 / SECOND_ORDER) + last[:, 2:34, 2:66]
    gradient = gradient.transpose(1, 2, 0).reshape(CX, CY * NZ)
    return gradient, density


def solution(mesh):
    return jax.shard_map(
        on_device,
        mesh=mesh,
        in_specs=(
            P("row", "col"),
            P(None, "row", "col"),
            P(),
            P(),
            P(("row", "col"), None),
            P(("row", "col")),
            P(("row", "col")),
            P(("row", "col")),
        ),
        out_specs=(P("row", "col"), P("row", "col")),
        check_vma=False,
    )
```

time: 782 us -> 204 us (0.26); the launches traced: 769 us -> 203 us
  local copies, waits for them, and re-layouts: 261 us -> 18.2 us
  matrix products: 179 us -> 0 us
  Pallas kernels: 0 us -> 138 us
  waiting for transfers between devices: 97.9 us -> 3.72 us
  other arithmetic: 72.5 us -> 0.2 us
  starting transfers between devices: 71.6 us -> 3.23 us
  blocking collectives: 82.3 us -> 38.8 us
    dot_general x42 -> x0, matrix products: 179 us -> none  [the longest x2 36.9 us: pull_group(): jnp.einsum('sayz,sby->sabz', picked, near_y, precision=PRECISE)]
    pallas_call x0 -> x10, Pallas kernels: none -> 138 us  [the longest x4 115 us: poisson(): pl.pallas_call(poisson_kernel, out_shape=jax.ShapeDtypeStruct((NZ, XH, 12...]
    all_to_all x10 -> x0, waiting for transfers between devices: 78.1 us -> none  [the longest x2 35.7 us: handover(): lax.all_to_all(payload, ('row', 'col'), split_axis=0, concat_axis=0, tile...]
    all_to_all x10 -> x0, starting transfers between devices: 55.3 us -> none  [the longest x4 24.3 us: by_half_columns(): lax.all_to_all(spectrum, 'col', split_axis=2, concat_axis=3, tiled=True)]
    reshape x12 -> x5, local copies, waits for them, and re-layouts: 56.9 us -> 7.19 us  [the longest x2 4.13 us: on_device(): delta.reshape(2, 16, CY, NZ).transpose(3, 1, 0, 2).reshape(NZ, 16, 128)]
    all_to_all x8 -> x2, blocking collectives: 82.3 us -> 38.8 us  [handover(): lax.all_to_all(payload.reshape(128, 8, 128), ('row', 'col'), split_axis=0...]
    transpose x18 -> x2, local copies, waits for them, and re-layouts: 45 us -> 2.69 us  [the longest x1 2.41 us: on_device(): delta.reshape(2, 16, CY, NZ).transpose(3, 1, 0, 2).reshape(NZ, 16, 128)]
    unnamed x193 -> x48, local copies, waits for them, and re-layouts: 41.5 us -> 8.1 us
  transfers between devices with their start and end apart: 26 -> 4, of which waited for: 15 -> 1; matrix products, arithmetic and copies ran while one was open for 7% -> 0% of each run, Pallas kernels for 0% -> 0%
where the time goes in v1:
time: 204 us; the launch traced here: 203 us
  Pallas kernels  138 us (68%)
  blocking collectives  38.8 us (19%)
  local copies, waits for them, and re-layouts  18.2 us (9%)
  waiting for transfers between devices  3.72 us (2%)
  starting transfers between devices  3.23 us (2%)
    pallas_call x4, Pallas kernels, poisson(): pl.pallas_call(poisson_kernel, out_shape=jax.ShapeDtypeStruct((NZ, XH, 12...  115 us
    all_to_all x2, blocking collectives, handover(): lax.all_to_all(payload.reshape(128, 8, 128), ('row', 'col'), split_axis=0...  38.8 us
    unnamed x48, local copies, waits for them, and re-layouts  8.1 us
    pallas_call x1, Pallas kernels, on_device(): local(paint_kernel, [shape(1024, 128), shape(3, 256, 128)], [pltpu.VMEM((...  8.07 us
    pallas_call x1, Pallas kernels, on_device(): local(weight_kernel, shape(NZ, 16, 128), [pltpu.VMEM((NZ, XH, 128), F32)]...  5.1 us
    pallas_call x1, Pallas kernels, on_device(): local(owner_kernel, [shape(CX, CY * NZ), shape(1024, 128)], [pltpu.VMEM((...  4.29 us
    reshape x2, local copies, waits for them, and re-layouts, on_device(): delta.reshape(2, 16, CY, NZ).transpose(3, 1, 0, 2).reshape(NZ, 16, 128)  4.13 us
  transfers between devices with their start and end apart: 4, of which 1 were waited for; matrix products, arithmetic and copies ran while one was open for 0% of the time, Pallas kernels for 0%

profile of v1, /device:TPU:1, one launch (start us, length us, event | category | flops | bytes accessed | tf_op | source)
XLA Modules:
  0.0 203.0 jit_solution(1455609070636224825)
XLA Ops:
  0.6 0.7 copy-done.22
  1.3 0.1 copy.27.az
  1.5 0.0 copy-done.19
  1.5 0.8 copy.24.owner_col
  2.3 1.5 copy.25.ax
  3.7 1.5 copy.26.ay
  5.2 2.3 %reshape.37 = f32[2,16,64,16]{3,2,1,0:T(8,128)} reshape(f32[32,1024]{1,0:T(8,128)} %param.18) | data formatting | bytes 262144 | tf_op jit(solution)/shard_map/reshape | solution.py:639
  7.5 2.4 %copy.23 = f32[16,16,2,64]{3,2,1,0:T(2,128)} copy(f32[16,16,2,64]{0,3,1,2:T(8,128)} %bitcast.22) | data formatting | bytes 262144 | tf_op jit(solution)/shard_map/transpose | solution.py:639
  10.0 1.8 reshape.38.src
  11.7 0.0 copy-done.3
  11.8 0.0 copy-done
  11.8 0.0 copy-start.4
  11.8 1.0 copy-done.4
  12.8 1.0 copy-done.6
  13.9 1.0 copy-done.8
  14.9 1.0 copy-done.10
  15.9 0.9 copy-done.14
  16.8 31.6 %poisson.4.first = f32[16,40,128]{2,1,0:T(8,128)S(1)} custom-call(f32[16,16,128]{2,1,0:T(8,128)S(1)} %copy-done.14, bf16[1024,256]{1,0:T(8,128)(2,1)S(1)} %copy-done.10, bf16[1024,256]{1,0:T(8,128)(2,1)S(1)} %copy-done.8, bf16[512,512]{1,0:T(8,128)(2,1)S(1)} %copy-done.6, bf16[512,512]{1,0:T(8,128)(2,1)S(1)} %copy-done.4, bf16[512,1024]{1,0:T(8,128)(2,1)S(1)} %copy-done.1, ...), custom_call_target="tpu_custom_call" | custom-call | tf_op jit(solution)/shard_map/poisson/pallas_call | solution.py:320
  48.5 2.8 %source.1.src = f32[16,16,128]{2,1,0:T(8,128)S(1)} custom-call(f32[16,40,128]{2,1,0:T(8,128)S(1)} %poisson.4.first), custom_call_target="tpu_custom_call" | custom-call | tf_op jit(solution)/shard_map/source/pallas_call | solution.py:641
  51.2 0.0 copy-start.16
  51.2 0.0 copy-start.18
  51.3 27.5 %poisson.5.second = f32[16,40,128]{2,1,0:T(8,128)S(1)} custom-call(f32[16,16,128]{2,1,0:T(8,128)S(1)} %source.1.src, bf16[1024,256]{1,0:T(8,128)(2,1)S(1)} %copy-done.11, bf16[1024,256]{1,0:T(8,128)(2,1)S(1)} %copy-done.8, bf16[512,512]{1,0:T(8,128)(2,1)S(1)} %copy-done.6, bf16[512,512]{1,0:T(8,128)(2,1)S(1)} %copy-done.4, bf16[512,1024]{1,0:T(8,128)(2,1)S(1)} %copy-done.1, ...), custom_call_target="tpu_custom_call" | custom-call | tf_op jit(solution)/shard_map/poisson/pallas_call | solution.py:320
  78.8 0.0 copy-start.13
  78.8 8.1 %paint.1 = (f32[1024,128]{1,0:T(8,128)S(1)}, f32[3,256,128]{2,1,0:T(8,128)S(1)}) custom-call(f32[16,40,128]{2,1,0:T(8,128)S(1)} %poisson.4.first, f32[16,40,128]{2,1,0:T(8,128)S(1)} %poisson.5.second, s32[1,256]{1,0:T(1,128)S(1)} %bitcast.20, s32[256,1]{1,0:T(8,128)S(1)} %copy-done.12, s32[256,1]{1,0:T(8,128)S(1)} %copy-done.15, s32[256,1]{1,0:T(8,128)S(1)} %copy-done.16, ...), custom_call_target="tpu_custom_call" | custom-call | tf_op jit(solution)/shard_map/paint/pallas_call | solution.py:643
  86.9 20.8 %all_to_all.10 = f32[128,8,128]{2,1,0:T(8,128)S(1)} all-to-all(f32[128,8,128]{2,1,0:T(8,128)S(1)} %bitcast.18), channel_id=1, replica_groups=mesh['row'=16,'col'=8] {'row','col'}, dimensions={0} | all-to-all | bytes 1048576 | tf_op jit(solution)/shard_map/all_to_all | solution.py:620
  107.7 0.6 copy-done.20
  108.4 0.0 copy-done.21
  108.4 4.3 %owner.1 = (f32[32,1024]{1,0:T(8,128)}, f32[1024,128]{1,0:T(8,128)S(1)}) custom-call(f32[8]{0:T(128)S(1)} %copy-done.20, f32[8]{0:T(128)S(1)} %copy-done.21, f32[1024,128]{1,0:T(8,128)S(1)} %bitcast.17, s32[8,32,1024]{2,1,0:T(8,128)S(1)} %copy-done.13), custom_call_target="tpu_custom_call" | custom-call | tf_op jit(solution)/shard_map/owner/pallas_call | solution.py:651
  112.7 0.0 copy-start.17
  112.7 18.0 %all_to_all.11 = f32[128,8,128]{2,1,0:T(8,128)S(1)} all-to-all(f32[128,8,128]{2,1,0:T(8,128)S(1)} %bitcast.19), channel_id=1, replica_groups=mesh['row'=16,'col'=8] {'row','col'}, dimensions={0} | all-to-all | bytes 1048576 | tf_op jit(solution)/shard_map/all_to_all | solution.py:620
  130.7 2.5 %force.1 = (f32[4,64,128]{2,1,0:T(8,128)S(1)}, f32[4,64,128]{2,1,0:T(8,128)S(1)}, f32[4,64,128]{2,1,0:T(8,128)S(1)}) custom-call(f32[1024,128]{1,0:T(8,128)S(1)} %bitcast.16, s32[1,256]{1,0:T(1,128)S(1)} %bitcast.21, s32[256,1]{1,0:T(8,128)S(1)} %copy-done.12, s32[256,1]{1,0:T(8,128)S(1)} %copy.27.az, bf16[256,512]{1,0:T(8,128)(2,1)S(1)} %copy-done.17, ...), custom_call_target="tpu_custom_call" | custom-call | tf_op jit(solution)/shard_map/force/pallas_call | solution.py:660
  133.3 0.1 slice_bitcast_fusion
  133.4 0.9 collective-permute-start.1
  134.2 0.6 collective-permute-start
  134.8 1.5 collective-permute-start.3
  136.4 0.2 collective-permute-start.2
  136.6 3.7 %collective-permute-done = f32[64,16]{1,0:T(8,128)S(1)} collective-permute-done((f32[64,16]{1,0:T(8,128)S(1)}, f32[64,16]{1,0:T(8,128)S(1)}, u32[]{:S(2)}, u32[]{:S(2)}) %collective-permute-start) | collective-permute-done | bytes 4128 | tf_op jit(solution)/shard_map/ppermute | solution.py:629
  140.3 0.0 collective-permute-done.1
  140.3 0.1 pad.9.x_high
  140.4 0.0 collective-permute-done.3.y_high
  140.4 0.0 collective-permute-done.2.y_low
  140.4 0.5 divergence.1.src
  141.0 27.6 %poisson.6.pulled = f32[16,40,128]{2,1,0:T(8,128)S(1)} custom-call(f32[16,16,128]{2,1,0:T(8,128)S(1)} %divergence.1.src, bf16[1024,256]{1,0:T(8,128)(2,1)S(1)} %copy-done.11, bf16[1024,256]{1,0:T(8,128)(2,1)S(1)} %copy-done.9, bf16[512,512]{1,0:T(8,128)(2,1)S(1)} %copy-done.7, bf16[512,512]{1,0:T(8,128)(2,1)S(1)} %copy-done.5, ...), custom_call_target="tpu_custom_call" | custom-call | tf_op jit(solution)/shard_map/poisson/pallas_call | solution.py:320
  168.6 5.1 %weights.1.src = f32[16,16,128]{2,1,0:T(8,128)S(1)} custom-call(f32[16,40,128]{2,1,0:T(8,128)S(1)} %poisson.4.first, f32[16,40,128]{2,1,0:T(8,128)S(1)} %poisson.6.pulled), custom_call_target="tpu_custom_call" | custom-call | tf_op jit(solution)/shard_map/weights/pallas_call | solution.py:675
  173.7 28.0 %poisson.7 = f32[16,40,128]{2,1,0:T(8,128)S(1)} custom-call(f32[16,16,128]{2,1,0:T(8,128)S(1)} %weights.1.src, bf16[1024,256]{1,0:T(8,128)(2,1)S(1)} %copy-done.11, bf16[1024,256]{1,0:T(8,128)(2,1)S(1)} %copy-done.9, bf16[512,512]{1,0:T(8,128)(2,1)S(1)} %copy-done.7, bf16[512,512]{1,0:T(8,128)(2,1)S(1)} %copy-done.5, bf16[512,1024]{1,0:T(8,128)(2,1)S(1)} %copy-done.1, ...), custom_call_target="tpu_custom_call" | custom-call | tf_op jit(solution)/shard_map/poisson/pallas_call | solution.py:320
  201.7 0.2 add_bitcast_fusion
  201.9 0.3 copy.30
  202.2 0.8 copy.31
  (32 shorter events, 0.1 us)
Async XLA Ops:
  0.6 0.7 copy-start.22
  0.6 0.8 copy-start.19
  1.3 10.4 %copy-start.3 = (bf16[640,512]{1,0:T(8,128)(2,1)S(1)}, bf16[640,512]{1,0:T(8,128)(2,1)}, u32[]{:S(2)}) copy-start(bf16[640,512]{1,0:T(8,128)(2,1)} %constant.31.clone.refs_6_) | copy-start | bytes 1966084
  5.2 6.6 %copy-start.1 = (bf16[512,1024]{1,0:T(8,128)(2,1)S(1)}, bf16[512,1024]{1,0:T(8,128)(2,1)}, u32[]{:S(2)}) copy-start(bf16[512,1024]{1,0:T(8,128)(2,1)} %constant.29.clone.refs_4_) | copy-start | bytes 3145732
  7.5 4.2 %copy-start = (bf16[512,1024]{1,0:T(8,128)(2,1)S(1)}, bf16[512,1024]{1,0:T(8,128)(2,1)}, u32[]{:S(2)}) copy-start(bf16[512,1024]{1,0:T(8,128)(2,1)} %constant.30.clone.refs_5_) | copy-start | bytes 3145732
  7.5 4.2 %copy-start.2 = (bf16[640,512]{1,0:T(8,128)(2,1)S(1)}, bf16[640,512]{1,0:T(8,128)(2,1)}, u32[]{:S(2)}) copy-start(bf16[640,512]{1,0:T(8,128)(2,1)} %constant.32.clone.refs_7_) | copy-start | bytes 1966084
  11.8 1.0 copy-start.4
  12.8 1.0 copy-start.6
  13.9 1.0 copy-start.8
  14.9 1.0 copy-start.10
  15.9 0.9 copy-start.14
  16.8 34.4 %copy-start.11 = (bf16[1024,256]{1,0:T(8,128)(2,1)S(1)}, bf16[1024,256]{1,0:T(8,128)(2,1)}, u32[]{:S(2)}) copy-start(bf16[1024,256]{1,0:T(8,128)(2,1)} %constant.25.clone.refs_0_) | copy-start | bytes 1572868
  51.2 27.6 %copy-start.12 = (s32[256,1]{1,0:T(8,128)S(1)}, s32[256,1]{1,0:T(8,128)}, u32[]{:S(2)}) copy-start(s32[256,1]{1,0:T(8,128)} %copy.24.owner_col) | copy-start | bytes 3076
  51.2 27.6 %copy-start.15 = (s32[256,1]{1,0:T(8,128)S(1)}, s32[256,1]{1,0:T(8,128)}, u32[]{:S(2)}) copy-start(s32[256,1]{1,0:T(8,128)} %copy.25.ax) | copy-start | bytes 3076
  51.2 27.6 %copy-start.16 = (s32[256,1]{1,0:T(8,128)S(1)}, s32[256,1]{1,0:T(8,128)}, u32[]{:S(2)}) copy-start(s32[256,1]{1,0:T(8,128)} %copy.26.ay) | copy-start | bytes 3076
  51.2 27.6 %copy-start.18 = (bf16[512,256]{1,0:T(8,128)(2,1)S(1)}, bf16[512,256]{1,0:T(8,128)(2,1)}, u32[]{:S(2)}) copy-start(bf16[512,256]{1,0:T(8,128)(2,1)} %constant.33.clone.spread) | copy-start | bytes 786436
  78.8 28.9 %copy-start.13 = (s32[8,32,1024]{2,1,0:T(8,128)S(1)}, s32[8,32,1024]{2,1,0:T(8,128)}, u32[]{:S(2)}) copy-start(s32[8,32,1024]{2,1,0:T(8,128)} %counts.1) | copy-start | bytes 3145732
  107.7 0.7 copy-start.20
  107.7 0.7 copy-start.21
  112.7 18.0 %copy-start.17 = (bf16[256,512]{1,0:T(8,128)(2,1)S(1)}, bf16[256,512]{1,0:T(8,128)(2,1)}, u32[]{:S(2)}) copy-start(bf16[256,512]{1,0:T(8,128)(2,1)} %constant.34.clone.spread_t) | copy-start | bytes 786436
  130.7 10.2 %copy-start.9 = (bf16[1024,256]{1,0:T(8,128)(2,1)S(1)}, bf16[1024,256]{1,0:T(8,128)(2,1)}, u32[]{:S(2)}) copy-start(bf16[1024,256]{1,0:T(8,128)(2,1)} %constant.26.clone.refs_1_) | copy-start | bytes 1572868
  133.4 7.0 %collective-permute-start.1 = (f32[64,16]{1,0:T(8,128)S(1)}, f32[64,16]{1,0:T(8,128)S(1)}, u32[]{:S(2)}, u32[]{:S(2)}) collective-permute-start(f32[64,16]{1,0:T(8,128)S(1)} %get-tuple-element.20), channel_id=1, source_target_pairs={{8,0},{16,8},{24,16},{32,24},{40,32},{48,40},{56,48},{64,56},{72,6... | collective-permute-start | bytes 12296 | tf_op jit(solution)/shard_map/ppermute | solution.py:629
  134.2 6.1 %collective-permute-start = (f32[64,16]{1,0:T(8,128)S(1)}, f32[64,16]{1,0:T(8,128)S(1)}, u32[]{:S(2)}, u32[]{:S(2)}) collective-permute-start(f32[64,16]{1,0:T(8,128)S(1)} %get-tuple-element.21), channel_id=1, source_target_pairs={{0,8},{8,16},{16,24},{24,32},{32,40},{40,48},{48,56},{56,64},{64,7... | collective-permute-start | bytes 12296 | tf_op jit(solution)/shard_map/ppermute | solution.py:629
  134.8 5.6 %collective-permute-start.3 = (f32[4,1,128]{2,1,0:T(1,128)S(1)}, f32[4,1,128]{2,1,0:T(1,128)S(1)}, u32[]{:S(2)}, u32[]{:S(2)}) collective-permute-start(f32[4,1,128]{2,1,0:T(1,128)S(1)} %get-tuple-element.18), channel_id=1, source_target_pairs={{1,0},{2,1},{3,2},{4,3},{5,4},{6,5},{7,6},{0,7},{9,8},{10,9},{11,1... | collective-permute-start | bytes 6152 | tf_op jit(solution)/shard_map/ppermute | solution.py:629
  136.4 4.6 %copy-start.5 = (bf16[512,512]{1,0:T(8,128)(2,1)S(1)}, bf16[512,512]{1,0:T(8,128)(2,1)}, u32[]{:S(2)}) copy-start(bf16[512,512]{1,0:T(8,128)(2,1)} %constant.28.clone.refs_3_) | copy-start | bytes 1572868
  136.4 4.6 %copy-start.7 = (bf16[512,512]{1,0:T(8,128)(2,1)S(1)}, bf16[512,512]{1,0:T(8,128)(2,1)}, u32[]{:S(2)}) copy-start(bf16[512,512]{1,0:T(8,128)(2,1)} %constant.27.clone.refs_2_) | copy-start | bytes 1572868
  136.4 4.0 %collective-permute-start.2 = (f32[4,1,128]{2,1,0:T(1,128)S(1)}, f32[4,1,128]{2,1,0:T(1,128)S(1)}, u32[]{:S(2)}, u32[]{:S(2)}) collective-permute-start(f32[4,1,128]{2,1,0:T(1,128)S(1)} %get-tuple-element.19), channel_id=1, source_target_pairs={{0,1},{1,2},{2,3},{3,4},{4,5},{5,6},{6,7},{7,0},{8,9},{9,10},{10,1... | collective-permute-start | bytes 6152 | tf_op jit(solution)/shard_map/ppermute | solution.py:629

commit v2 on v1

--- a/solution.py
+++ b/solution.py
@@ -223,42 +223,7 @@
         copy.wait_recv()
 
 
-def poisson_kernel(
-    src, *refs
-):
-    tables = refs[:8]
-    out = refs[8]
-    mo, r1, pk, r2, zb, r3, xb, r4 = refs[9:17]
-    held = refs[17:25]
-    tsem, s1, q1, s2, q2, s3, q3, s4, q4, own = refs[25:]
-    row, col = lax.axis_index("row"), lax.axis_index("col")
-
-    barrier = pltpu.get_barrier_semaphore()
-    for k in range(1, NROW):
-        pl.semaphore_signal(
-            barrier, inc=1, device_id={"row": lax.rem(row + k, NROW)}, device_id_type=MESH
-        )
-    for k in range(1, NCOL):
-        pl.semaphore_signal(
-            barrier, inc=1, device_id={"col": lax.rem(col + k, NCOL)}, device_id_type=MESH
-        )
-    loads = [
-        pltpu.make_async_copy(t, h, tsem.at[i]) for i, (t, h) in enumerate(zip(tables, held))
-    ]
-    for load in loads:
-        load.start()
-    for s in range(2):
-        rows = pl.ds(8 * s, 8)
-        for m, value in enumerate(forward_z([src[z, rows, :] for z in range(16)])):
-            mo[m, rows, :] = value
-    pl.semaphore_wait(barrier, NROW + NCOL - 2)
-
-    low_half = lanes((256, 128)) < 64
-    state1 = exchange(NROW, row, "row", mo, r1, s1, q1, own.at[0])
-    for load in loads:
-        load.wait()
-    fxh, fxl, fyh, fyl, gyh, gyl, gxh, gxl = held
-
+def modes_factor(row, col):
     kx = lanes((64, GRID), 0) + col * 64
     ky = lanes((64, GRID), 1)
     kx = jnp.where(kx <= GRID // 2, kx, kx - GRID // 2).astype(F32) * (2.0 * math.pi / GRID)
@@ -266,8 +231,18 @@
     kz = jnp.where(row <= NZ // 2, row, row - NZ // 2)
     kz = jnp.full((64, GRID), kz, jnp.int32).astype(F32) * (2.0 * math.pi / NZ)
     square = kx * kx + ky * ky + kz * kz
-    factor = jnp.where(square > 0, -1.0 / jnp.where(square > 0, square, 1.0), 0.0)
-
+    return jnp.where(square > 0, -1.0 / jnp.where(square > 0, square, 1.0), 0.0)
+
+
+def solve(place, buffers, semaphores, held, factor, out, pending, ready=None):
+    row, col = place
+    mo, r1, pk, r2, zb, r3, xb, r4 = buffers
+    s1, q1, s2, q2, s3, q3, s4, q4, own = semaphores
+    fxh, fxl, fyh, fyl, gyh, gyl, gxh, gxl = held
+    low_half = lanes((256, 128)) < 64
+    state1 = exchange(NROW, row, "row", mo, r1, s1, q1, own.at[0])
+    if ready is not None:
+        ready()
     arrive(state1)
     t = left_product(fxh[...], fxl[...], r1[...].reshape(256, 128))
     packed = jnp.where(low_half, t[:256], t[256:512]) + roll(
@@ -285,7 +260,7 @@
     full = jnp.concatenate(
         [jnp.concatenate(top, axis=1), jnp.concatenate(bottom, axis=1)], axis=0
     )
-    modes = right_product(full, fyh[...], fyl[...]) * factor
+    modes = right_product(full, fyh[...], fyl[...]) * factor[...]
     back = right_product(modes, gyh[...], gyl[...])
     for c in range(NCOL):
         zb[c] = back[:, 128 * c : 128 * (c + 1)]
@@ -299,35 +274,93 @@
         for z, value in enumerate(inverse_z([r4[m, rows, :] for m in range(16)])):
             out[z, rows, :] = value
     for state in (state1, state2, state3, state4):
-        for copy in state[0]:
-            copy.wait_send()
+        pending.extend(state[0])
+
+
+def to_modes(src, mo):
+    for s in range(2):
+        rows = pl.ds(8 * s, 8)
+        for m, value in enumerate(forward_z([src[z, rows, :] for z in range(16)])):
+            mo[m, rows, :] = value
+
+
+def delta_modes(delta, tzh, tzl, mo):
+    d = delta[...]
+    t = right_product(
+        jnp.concatenate([d[:, 256 * q : 256 * (q + 1)] for q in range(4)], axis=0),
+        tzh[...],
+        tzl[...],
+    )
+    slot = lanes((16, 128)) // 16
+    for m in range(16):
+        part = 128 * (m // 8)
+        value = None
+        for h in range(2):
+            for q in range(4):
+                piece = t[32 * q + 16 * h : 32 * q + 16 * h + 16, part : part + 128]
+                piece = roll(piece, 16 * (4 * h + q - m % 8), 1)
+                value = piece if value is None else jnp.where(slot == 4 * h + q, piece, value)
+        mo[m] = value
+
+
+def handover(row, col, src, dst, send, recv, own):
+    me = row * NCOL + col
+
+    @pl.loop(1, 128)
+    def _(k):
+        peer = lax.rem(me + k, 128)
+        pltpu.make_async_remote_copy(
+            src_ref=src.at[peer],
+            dst_ref=dst.at[me],
+            send_sem=send,
+            recv_sem=recv,
+            device_id={"row": peer // NCOL, "col": lax.rem(peer, NCOL)},
+            device_id_type=MESH,
+        ).start()
+
+    copy = pltpu.make_async_copy(src.at[me], dst.at[me], own)
+    copy.start()
+    copy.wait()
+    all_of_them = pltpu.make_async_remote_copy(
+        src_ref=src.at[pl.ds(0, 127)],
+        dst_ref=dst.at[pl.ds(0, 127)],
+        send_sem=send,
+        recv_sem=recv,
+        device_id={"col": lax.rem(col + 1, NCOL)},
+        device_id_type=MESH,
+    )
+    all_of_them.wait_recv()
+    return all_of_them
+
+
+def neighbours(row, col, fx, fy, x_low, x_high, y_low, y_high, sems, pending):
+    copies = []
+    for i, (axis, peer, src, dst) in enumerate(
+        (
+            ("row", lax.rem(row + 1, NROW), fx.at[3], x_low),
+            ("row", lax.rem(row + NROW - 1, NROW), fx.at[0], x_high),
+            ("col", lax.rem(col + 1, NCOL), fy.at[:, pl.ds(56, 8)], y_low),
+            ("col", lax.rem(col + NCOL - 1, NCOL), fy.at[:, pl.ds(0, 8)], y_high),
+        )
+    ):
+        copies.append(
+            pltpu.make_async_remote_copy(
+                src_ref=src,
+                dst_ref=dst,
+                send_sem=sems.at[0, i],
+                recv_sem=sems.at[1, i],
+                device_id={axis: peer},
+                device_id_type=MESH,
+            )
+        )
+        copies[-1].start()
+    for copy in copies:
+        copy.wait_recv()
+    pending.extend(copies)
 
 
 VM = pl.BlockSpec(memory_space=pltpu.VMEM)
 ANY = pl.BlockSpec(memory_space=pl.ANY)
-
-
-def poisson(src, tables):
-    buffers = [(NROW, 16, 128), (NCOL, 32, 128), (NCOL, 64, 128), (NROW, XH, 128)]
-    scratch = []
-    for shape in buffers:
-        scratch += [pltpu.VMEM(shape, F32), pltpu.VMEM(shape, F32)]
-    scratch += [pltpu.VMEM(t.shape, BF16) for t in tables]
-    scratch += [pltpu.SemaphoreType.DMA((8,))]
-    for n in (NROW, NCOL, NCOL, NROW):
-        scratch += [pltpu.SemaphoreType.DMA((n,)), pltpu.SemaphoreType.DMA((n,))]
-    scratch += [pltpu.SemaphoreType.DMA((4,))]
-    return pl.pallas_call(
-        poisson_kernel,
-        out_shape=jax.ShapeDtypeStruct((NZ, XH, 128), F32),
-        in_specs=[VM] + [ANY] * 8,
-        out_specs=VM,
-        scratch_shapes=scratch,
-        compiler_params=pltpu.CompilerParams(
-            collective_id=0, has_side_effects=True, vmem_limit_bytes=40 << 20
-        ),
-        name="poisson",
-    )(src, *tables)
 
 
 def pack(f):
@@ -349,7 +382,7 @@
     return xx, yy, zz, xy, xz, yz
 
 
-def source_kernel(first, out):
+def source(first, out):
     @pl.loop(0, NZ)
     def _(z):
         xx, yy, zz, xy, xz, yz = curvatures(
@@ -390,8 +423,7 @@
     return along, down_
 
 
-def paint_kernel(first, second, owner_row, owner_col, ax, ay, az, spread, out, fracs, tz, tt):
-    zrows = [None, None, None]
+def paint(first, second, along, ax, ay, az, spread, out, fracs, tz, tt):
     piece = lanes((16, 128)) // 32
     for axis in range(3):
 
@@ -418,9 +450,8 @@
                 for v in range(1, 4):
                     block = jnp.where(piece == v, roll(quarter[v], 32 * (v - k), 1), block)
                 fracs[axis, pl.ds(16 * (4 * q + k), 16), :] = block
-    amount = az[...]
     for axis in range(3):
-        fracs[axis] = barrel(fracs[axis], amount)
+        fracs[axis] = barrel(fracs[axis], az)
     fx, fy, fz = fracs[0], fracs[1], fracs[2]
     fields = []
     for wx in (1.0 - fx, fx):
@@ -430,17 +461,16 @@
             fields.append(q - upper + group_roll(upper, 1))
     box = exact_right(jnp.concatenate(fields, axis=1), spread[...])
     lane = lanes((256, 256))
-    box = jnp.where(lane == 240, ax[...].astype(F32), box)
-    box = jnp.where(lane == 241, ay[...].astype(F32), box)
-    along, _ = slots(owner_row[...], owner_col[...])
+    box = jnp.where(lane == 240, ax.astype(F32), box)
+    box = jnp.where(lane == 241, ay.astype(F32), box)
     target = jnp.concatenate([along, along + 4], axis=1)
     table = jnp.where(lanes((1024, 512), 0) == target, 1.0, 0.0).astype(BF16)
     stacked = jnp.concatenate([box[:, :128], box[:, 128:]], axis=0)
-    out[...] = exact_left(table, stacked)
-
-
-def owner_kernel(nbar, bias, arrived, counts, density, back, dens, pulls):
-    data = arrived[...]
+    out[...] = exact_left(table, stacked).reshape(128, 8, 128)
+
+
+def own_cells(nbar, bias, arrived, counts, density, back, dens, pulls):
+    data = arrived[...].reshape(1024, 128)
     second = lanes((1024, 128), 0) // 4 % 2
     is_second = second == 1
 
@@ -500,14 +530,14 @@
         value = jnp.where(stay, t[:, :128] + t[:, 128:256], t[:, 256:384] + t[:, 384:])
         return barrel_16(value, (8 - amount) & 7)
 
-    back[...] = jnp.where(lane < 80, picked(2 * second, step), picked(1, side_step))
-
-
-def force_kernel(returned, owner_row, owner_col, az, spread_t, fracs, fx_out, fy_out, fz_out):
-    _, place = slots(owner_row[...], owner_col[...])
+    value = jnp.where(lane < 80, picked(2 * second, step), picked(1, side_step))
+    back[...] = value.reshape(128, 8, 128)
+
+
+def forces(returned, place, az, spread_t, fracs, fx_out, fy_out, fz_out):
     target = jnp.concatenate([place, place + 4], axis=0)
     table = jnp.where(lanes((512, 1024)) == target, 1.0, 0.0).astype(BF16)
-    t = exact_left(table, returned[...])
+    t = exact_left(table, returned[...].reshape(1024, 128))
     box = jnp.concatenate([t[:256], t[256:]], axis=1)
     corner = exact_right(box, spread_t[...])
     fx, fy, fz = fracs[0], fracs[1], fracs[2]
@@ -517,7 +547,7 @@
         change = group_roll(here, 15) - here
         along.append(here + fz * change)
         across.append(change)
-    amount = (16 - az[...]) & 15
+    amount = (16 - az) & 15
     force_x = (1.0 - fy) * (along[2] - along[0]) + fy * (along[3] - along[1])
     force_y = (1.0 - fx) * (along[1] - along[0]) + fx * (along[3] - along[2])
     force_z = (1.0 - fx) * ((1.0 - fy) * across[0] + fy * across[1]) + fx * (
@@ -535,19 +565,25 @@
                 out[q, pl.ds(v, 16, stride=4), :] = value
 
 
-def divergence_kernel(fx, fy, fz, x_low, x_high, y_low, y_high, out, tz):
+def divergence(fx, fy, fz, x_low, x_high, y_low, y_high, out, tz):
     def wide(ref):
         return jnp.concatenate([ref[q] for q in range(4)], axis=1)
 
+    def four(value):
+        return jnp.concatenate([value] * 4, axis=1)
+
+    def edge(ref, i):
+        return jnp.concatenate([ref[q, i : i + 1, :] for q in range(4)], axis=1)
+
     f = wide(fx)
     lane = lanes((64, 512))
-    before = jnp.where(lane < 16, x_low[...], roll(f, 16, 1))
-    after = jnp.where(lane >= 496, x_high[...], roll(f, -16, 1))
+    before = jnp.where(lane < 16, four(roll(x_low[...], 16, 1)), roll(f, 16, 1))
+    after = jnp.where(lane >= 496, four(roll(x_high[...], 112, 1)), roll(f, -16, 1))
     total = after - before
     g = wide(fy)
     line = lanes((64, 512), 0)
-    before = jnp.where(line == 0, wide(y_low), roll(g, 1, 0))
-    after = jnp.where(line == 63, wide(y_high), roll(g, -1, 0))
+    before = jnp.where(line == 0, edge(y_low, 7), roll(g, 1, 0))
+    after = jnp.where(line == 63, edge(y_high, 0), roll(g, -1, 0))
     total = total + (after - before)
     h = wide(fz)
     z = lane % 16
@@ -564,7 +600,7 @@
         )
 
 
-def weight_kernel(first, pulled, out, part, wzz, wxz, wyz):
+def weights(first, pulled, out, part, wzz, wxz, wyz):
     @pl.loop(0, NZ)
     def _(z):
         xx, yy, zz, xy, xz, yz = curvatures(
@@ -595,93 +631,153 @@
         )
 
 
-def local(kernel, outs, scratch=(), smem=0, n=0, name=None):
-    many = isinstance(outs, (list, tuple))
-    return pl.pallas_call(
-        kernel,
-        out_shape=outs,
-        in_specs=[pl.BlockSpec(memory_space=pltpu.SMEM)] * smem + [VM] * (n - smem),
-        out_specs=[VM] * len(outs) if many else VM,
-        scratch_shapes=list(scratch),
-        compiler_params=pltpu.CompilerParams(vmem_limit_bytes=40 << 20),
-        name=name,
-    )
-
-
-def shape(*s):
-    return jax.ShapeDtypeStruct(s, F32)
-
-
-TABLES = make_tables()
-SPREAD = make_spread()
-
-
-def handover(payload):
-    moved = lax.all_to_all(
-        payload.reshape(128, 8, 128), ("row", "col"), split_axis=0, concat_axis=0, tiled=True
-    )
-    return moved.reshape(1024, 128)
-
-
-def neighbours(low, high, axis, count):
-    forward = [(i, (i + 1) % count) for i in range(count)]
-    backward = [((i + 1) % count, i) for i in range(count)]
-    return lax.ppermute(high, axis, forward), lax.ppermute(low, axis, backward)
+def columns(rows):
+    stack = jnp.concatenate([r.astype(F32) for r in rows] + [jnp.zeros((124, 256), F32)], axis=0)
+    turned = jnp.concatenate([jnp.transpose(stack[:, :128]), jnp.transpose(stack[:, 128:])], axis=0)
+    return [turned[:, i : i + 1].astype(jnp.int32) for i in range(len(rows))]
+
+
+N_TABLES = 12
+
+
+def whole_kernel(nbar, bias, delta, owner, anchor_x, anchor_y, anchor_z, *refs):
+    counts_far, tables = refs[0], refs[1 : 1 + N_TABLES]
+    gradient, density = refs[1 + N_TABLES : 3 + N_TABLES]
+    rest = list(refs[3 + N_TABLES :])
+
+    def take(n):
+        taken, rest[:] = rest[:n], rest[n:]
+        return taken
+
+    held, (counts,) = take(N_TABLES), take(1)
+    buffers = [take(8) for _ in range(4)]
+    first, second, pulled, last, part, wzz, wxz, wyz = take(8)
+    src, factor, fracs, tz, tt = take(5)
+    payload, arrived, back, returned, dens, pulls = take(6)
+    fx, fy, fz, x_low, x_high, y_low, y_high = take(7)
+    table_sem, *exchange_sems, own, hand_sem, edge_sem = rest
+    row, col = lax.axis_index("row"), lax.axis_index("col")
+    me = row * NCOL + col
+    pending = []
+
+    def semaphores(i):
+        return [s.at[i] for s in exchange_sems] + [own.at[i]]
+
+    barrier = pltpu.get_barrier_semaphore()
+
+    @pl.loop(1, 128)
+    def _(k):
+        peer = lax.rem(me + k, 128)
+        pl.semaphore_signal(
+            barrier,
+            inc=1,
+            device_id={"row": peer // NCOL, "col": lax.rem(peer, NCOL)},
+            device_id_type=MESH,
+        )
+
+    loads = [
+        pltpu.make_async_copy(t, h, table_sem.at[i])
+        for i, (t, h) in enumerate(zip((*tables, counts_far), (*held, counts)))
+    ]
+    for load in loads:
+        load.start()
+    tzh, tzl, *main, spread, spread_t = held
+    loads[0].wait()
+    loads[1].wait()
+    delta_modes(delta, tzh, tzl, buffers[0][0])
+    pl.semaphore_wait(barrier, 127)
+
+    def ready():
+        factor[...] = modes_factor(row, col)
+        for load in loads[2:]:
+            load.wait()
+
+    place = (row, col)
+    solve(place, buffers[0], semaphores(0), main, factor, first, pending, ready)
+    source(first, src)
+    to_modes(src, buffers[1][0])
+    solve(place, buffers[1], semaphores(1), main, factor, second, pending)
+    owner_row = owner[...]
+    rows = (owner_row, anchor_x[...], anchor_y[...], anchor_z[...])
+    owner_col, ax, ay, az = columns(rows)
+    along, down_rows = slots(owner_row, owner_col)
+    paint(first, second, along, ax, ay, az, spread, payload, fracs, tz, tt)
+    pending.append(handover(row, col, payload, arrived, hand_sem.at[0], hand_sem.at[1], hand_sem.at[2]))
+    own_cells(nbar, bias, arrived, counts, density, back, dens, pulls)
+    pending.append(handover(row, col, back, returned, hand_sem.at[3], hand_sem.at[4], hand_sem.at[5]))
+    forces(returned, down_rows, az, spread_t, fracs, fx, fy, fz)
+    neighbours(row, col, fx, fy, x_low, x_high, y_low, y_high, edge_sem, pending)
+    divergence(fx, fy, fz, x_low, x_high, y_low, y_high, src, tz)
+    to_modes(src, buffers[2][0])
+    solve(place, buffers[2], semaphores(2), main, factor, pulled, pending)
+    weights(first, pulled, src, part, wzz, wxz, wyz)
+    to_modes(src, buffers[3][0])
+    solve(place, buffers[3], semaphores(3), main, factor, last, pending)
+
+    @pl.loop(0, NZ)
+    def _(z):
+        value = pulled[z] * (1.0 / SECOND_ORDER) + last[z]
+        gradient[z] = roll(roll(value, -2, 0)[0:32], -2, 1)
+
+    for copy in pending:
+        copy.wait_send()
+
+
+def delta_table():
+    t = np.zeros((16, 16, 16, 16))
+    for y in range(16):
+        t[y, :, :, y] = ZB.T
+    return two_terms(t.reshape(256, 256))
+
+
+def spread_tables():
+    spread = make_spread()
+    return [spread.astype(jnp.bfloat16), spread.T.copy().astype(jnp.bfloat16)]
+
+
+TABLES = [*delta_table(), *make_tables(), *spread_tables()]
 
 
 def on_device(delta, counts, nbar, bias, owner, anchor_x, anchor_y, anchor_z):
     tables = [jnp.asarray(t) for t in TABLES]
-    spread = jnp.asarray(SPREAD, BF16)
-    spread_t = jnp.asarray(SPREAD.T, BF16)
-    owner_row, owner_col = owner.reshape(1, 256), owner
-    ax, ay, az = (a.reshape(256, 1) for a in (anchor_x, anchor_y, anchor_z))
-
-    src = delta.reshape(2, 16, CY, NZ).transpose(3, 1, 0, 2).reshape(NZ, 16, 128)
-    first = poisson(src, tables)
-    src = local(source_kernel, shape(NZ, 16, 128), n=1, name="source")(first)
-    second = poisson(src, tables)
-    payload, fracs = local(
-        paint_kernel,
-        [shape(1024, 128), shape(3, 256, 128)],
-        [pltpu.VMEM((512, 128), F32), pltpu.VMEM((4, 64, 128), F32)],
-        n=8,
-        name="paint",
-    )(first, second, owner_row, owner_col, ax, ay, az, spread)
-    arrived = handover(payload)
-    density, back = local(
-        owner_kernel,
-        [shape(CX, CY * NZ), shape(1024, 128)],
-        [pltpu.VMEM((256, 128), F32), pltpu.VMEM((256, 128), F32)],
-        smem=2,
-        n=4,
-        name="owner",
-    )(nbar, bias, arrived, counts)
-    returned = handover(back)
-    fx, fy, fz = local(force_kernel, [shape(4, CY, 128)] * 3, n=6, name="force")(
-        returned, owner_row, owner_col, az, spread_t, fracs
-    )
-    x_low, x_high = neighbours(fx[0, :, :16], fx[3, :, 112:], "row", NROW)
-    y_low, y_high = neighbours(fy[:, :1], fy[:, 63:], "col", NCOL)
-    x_low = jnp.pad(x_low, ((0, 0), (0, 496)))
-    x_high = jnp.pad(x_high, ((0, 0), (496, 0)))
-    src = local(
-        divergence_kernel,
-        shape(NZ, 16, 128),
-        [pltpu.VMEM((512, 128), F32)],
-        n=7,
-        name="divergence",
-    )(fx, fy, fz, x_low, x_high, y_low, y_high)
-    pulled = poisson(src, tables)
-    src = local(
-        weight_kernel,
-        shape(NZ, 16, 128),
-        [pltpu.VMEM((NZ, XH, 128), F32)] * 4,
-        n=2,
-        name="weights",
-    )(first, pulled)
-    last = poisson(src, tables)
-    gradient = pulled[:, 2:34, 2:66] * (1.0 / SECOND_ORDER) + last[:, 2:34, 2:66]
-    gradient = gradient.transpose(1, 2, 0).reshape(CX, CY * NZ)
+    flat = [a.reshape(1, 256) for a in (owner, anchor_x, anchor_y, anchor_z)]
+    field = pltpu.VMEM((NZ, XH, 128), F32)
+    hand = pltpu.VMEM((128, 8, 128), F32)
+    scratch = [pltpu.VMEM(t.shape, BF16) for t in tables] + [pltpu.VMEM(counts.shape, jnp.int32)]
+    for _ in range(4):
+        for s in ((NROW, 16, 128), (NCOL, 32, 128), (NCOL, 64, 128), (NROW, XH, 128)):
+            scratch += [pltpu.VMEM(s, F32), pltpu.VMEM(s, F32)]
+    scratch += [field] * 8
+    scratch += [pltpu.VMEM((NZ, 16, 128), F32), pltpu.VMEM((64, GRID), F32)]
+    scratch += [pltpu.VMEM((3, 256, 128), F32), pltpu.VMEM((512, 128), F32)]
+    scratch += [pltpu.VMEM((4, 64, 128), F32)]
+    scratch += [hand] * 4 + [pltpu.VMEM((256, 128), F32)] * 2
+    scratch += [pltpu.VMEM((4, 64, 128), F32)] * 3
+    scratch += [pltpu.VMEM((64, 128), F32)] * 2 + [pltpu.VMEM((4, 8, 128), F32)] * 2
+    scratch += [pltpu.SemaphoreType.DMA((len(tables) + 1,))]
+    for n in (NROW, NCOL, NCOL, NROW):
+        scratch += [pltpu.SemaphoreType.DMA((4, n)), pltpu.SemaphoreType.DMA((4, n))]
+    scratch += [
+        pltpu.SemaphoreType.DMA((4, 4)),
+        pltpu.SemaphoreType.DMA((6,)),
+        pltpu.SemaphoreType.DMA((2, 4)),
+    ]
+    smem = pl.BlockSpec(memory_space=pltpu.SMEM)
+    gradient, density = pl.pallas_call(
+        whole_kernel,
+        out_shape=[
+            jax.ShapeDtypeStruct((NZ, CX, 128), F32),
+            jax.ShapeDtypeStruct((CX, CY * NZ), F32),
+        ],
+        in_specs=[smem] * 2 + [VM] * 5 + [ANY] * (1 + len(tables)),
+        out_specs=[VM, VM],
+        scratch_shapes=scratch,
+        compiler_params=pltpu.CompilerParams(
+            collective_id=0, has_side_effects=True, vmem_limit_bytes=60 << 20
+        ),
+        name="whole",
+    )(nbar, bias, delta, *flat, counts, *tables)
+    gradient = gradient[:, :, :CY].transpose(1, 2, 0).reshape(CX, CY * NZ)
     return gradient, density
 
 

time: 204 us -> 164 us (0.80)
  blocking collectives: 38.8 us -> 0 us
  Pallas kernels: 138 us -> 160 us
  local copies, waits for them, and re-layouts: 18.2 us -> 2.8 us
  waiting for transfers between devices: 3.72 us -> 0 us
  starting transfers between devices: 3.23 us -> 0 us
    all_to_all x2 -> x0, blocking collectives: 38.8 us -> none  [handover(): lax.all_to_all(payload.reshape(128, 8, 128), ('row', 'col'), split_axis=0...]
    pallas_call x10 -> x1, Pallas kernels: 138 us -> 160 us  [on_device(): pl.pallas_call(whole_kernel, out_shape=[jax.ShapeDtypeStruct((NZ, CX, 128...]
    reshape x5 -> x0, local copies, waits for them, and re-layouts: 7.19 us -> none  [the longest x2 4.13 us: on_device(): delta.reshape(2, 16, CY, NZ).transpose(3, 1, 0, 2).reshape(NZ, 16, 128)]
    unnamed x48 -> x4, local copies, waits for them, and re-layouts: 8.1 us -> 1.55 us
    ppermute x4 -> x0, waiting for transfers between devices: 3.72 us -> none  [the longest x2 3.71 us: neighbours(): lax.ppermute(high, axis, forward)]
    ppermute x4 -> x0, starting transfers between devices: 3.23 us -> none  [the longest x2 2.39 us: neighbours(): lax.ppermute(low, axis, backward)]
  transfers between devices with their start and end apart: 4 -> 0, of which waited for: 1 -> 0; matrix products, arithmetic and copies ran while one was open for 0% -> 0% of each run, Pallas kernels for 0% -> 0%
where the time goes in v2:
time: 164 us; the launch traced here: 163 us
  Pallas kernels  160 us (98%)
  local copies, waits for them, and re-layouts  2.8 us (2%)
    pallas_call x1, Pallas kernels, on_device(): pl.pallas_call(whole_kernel, out_shape=[jax.ShapeDtypeStruct((NZ, CX, 128...  160 us

profile of v2, /device:TPU:1, one launch (start us, length us, event | category | flops | bytes accessed | tf_op | source)
XLA Modules:
  0.0 163.3 jit_solution(2344133550777551663)
XLA Ops:
  0.6 159.9 %whole.1 = (f32[16,32,128]{2,1,0:T(8,128)}, f32[32,1024]{1,0:T(8,128)}) custom-call(f32[8]{0:T(128)} %nbar.1, f32[8]{0:T(128)} %bias.1, f32[32,1024]{1,0:T(8,128)} %delta.1, s32[1,256]{1,0:T(1,128)} %bitcast.8, s32[1,256]{1,0:T(1,128)} %bitcast.9, s32[1,256]{1,0:T(1,128)} %bitcast.10, s32[1,256]{1,0:T(1,128)} %bitcast.11, s32[8,32,1024]{2,1,0:T(8,128)} %refs_0_.1, ...), custom_call_target="tpu_custom_call" | custom-call | tf_op jit(solution)/shard_map/whole/pallas_call | solution.py:766
  160.5 1.0 slice_bitcast_fusion
  161.5 0.3 copy.22
  161.8 0.0 copy-start
  161.8 0.8 copy.23
  162.6 0.1 copy-done
  162.7 0.7 copy.25
Async XLA Ops:
  161.8 0.9 copy-start

commit v3 on v2

--- a/solution.py
+++ b/solution.py
@@ -58,10 +58,12 @@
     fy = basis.T
     gy = np.zeros((GRID, NCOL, 128))
     for c in range(NCOL):
-        gy[:, c, :68] = basis[:, (CY * c - 2 + np.arange(68)) % GRID]
+        for y in range(-2, CY + 2):
+            gy[:, c, y % 128] = basis[:, (CY * c + y) % GRID]
     gx = np.zeros((NROW, XH, GRID))
     for r in range(NROW):
-        gx[r, :36] = basis[:, (CX * r - 2 + np.arange(36)) % GRID].T
+        for x in range(-2, CX + 2):
+            gx[r, x % XH] = basis[:, (CX * r + x) % GRID]
     tables = []
     for t in (fx, fy, gy.reshape(GRID, NCOL * 128), gx.reshape(NROW * XH, GRID)):
         tables.extend(two_terms(t))
@@ -187,9 +189,14 @@
     return out
 
 
+def distance(n, k):
+    around = lambda d: min(d, 4 - d)
+    return around(k % 4) + around(k // 4) if n == NROW else around(k // 2)
+
+
 def exchange(n, me, axis, src, dst, send, recv, own):
     sends, recvs = [], []
-    for k in range(1, n):
+    for k in sorted(range(1, n), key=lambda k: -distance(n, k)):
         peer = lax.rem(me + k, n)
         origin = lax.rem(me + n - k, n)
         copy = pltpu.make_async_remote_copy(
@@ -234,15 +241,15 @@
     return jnp.where(square > 0, -1.0 / jnp.where(square > 0, square, 1.0), 0.0)
 
 
-def solve(place, buffers, semaphores, held, factor, out, pending, ready=None):
+def solve(place, buffers, semaphores, held, factor, out, pending, fill=(None,) * 4):
     row, col = place
     mo, r1, pk, r2, zb, r3, xb, r4 = buffers
     s1, q1, s2, q2, s3, q3, s4, q4, own = semaphores
     fxh, fxl, fyh, fyl, gyh, gyl, gxh, gxl = held
     low_half = lanes((256, 128)) < 64
     state1 = exchange(NROW, row, "row", mo, r1, s1, q1, own.at[0])
-    if ready is not None:
-        ready()
+    if fill[0]:
+        fill[0]()
     arrive(state1)
     t = left_product(fxh[...], fxl[...], r1[...].reshape(256, 128))
     packed = jnp.where(low_half, t[:256], t[256:512]) + roll(
@@ -250,6 +257,8 @@
     )
     pk[...] = packed.reshape(NCOL, 32, 128)
     state2 = exchange(NCOL, col, "col", pk, r2, s2, q2, own.at[1])
+    if fill[1]:
+        fill[1]()
     arrive(state2)
     half = lanes((32, 128)) < 64
     top, bottom = [], []
@@ -265,11 +274,15 @@
     for c in range(NCOL):
         zb[c] = back[:, 128 * c : 128 * (c + 1)]
     state3 = exchange(NCOL, col, "col", zb, r3, s3, q3, own.at[2])
+    if fill[2]:
+        fill[2]()
     arrive(state3)
     xb[...] = left_product(gxh[...], gxl[...], r3[...].reshape(GRID, 128)).reshape(NROW, XH, 128)
     state4 = exchange(NROW, row, "row", xb, r4, s4, q4, own.at[3])
+    if fill[3]:
+        fill[3]()
     arrive(state4)
-    for s in range(5):
+    for s in range(5 if out is not None else 0):
         rows = pl.ds(8 * s, 8)
         for z, value in enumerate(inverse_z([r4[m, rows, :] for m in range(16)])):
             out[z, rows, :] = value
@@ -364,10 +377,7 @@
 
 
 def pack(f):
-    f = roll(f, -2, 0)
-    low = roll(f[0:16], -2, 1)
-    high = roll(f[16:32], 62, 1)
-    return jnp.where(lanes((16, 128)) < 64, low, high)
+    return jnp.where(lanes((16, 128)) < 64, f[0:16], roll(f[16:32], 64, 1))
 
 
 def curvatures(below, here, above):
@@ -383,12 +393,20 @@
 
 
 def source(first, out):
-    @pl.loop(0, NZ)
-    def _(z):
+    for z in range(NZ):
         xx, yy, zz, xy, xz, yz = curvatures(
             first[(z + 15) % 16], first[z], first[(z + 1) % 16]
         )
-        out[z] = pack(xx * yy + xx * zz + yy * zz - xy * xy - xz * xz - yz * yz)
+        out[z] = pack(xx * (yy + zz) + yy * zz - (xy * xy + xz * xz + yz * yz))
+
+
+def keep_curvatures(first, kept, zs):
+    for z in zs:
+        xx, yy, zz, xy, xz, yz = curvatures(
+            first[(z + 15) % 16], first[z], first[(z + 1) % 16]
+        )
+        for i, value in enumerate((yy + zz, xx + zz, xx + yy, -2.0 * xy, -2.0 * xz, -2.0 * yz)):
+            kept[i, z] = value
 
 
 def group_roll(x, s):
@@ -423,24 +441,31 @@
     return along, down_
 
 
-def paint(first, second, along, ax, ay, az, spread, out, fracs, tz, tt):
+def place_tables(along, down_rows, to_slot, from_slot):
+    target = jnp.concatenate([along, along + 4], axis=1)
+    for i in range(4):
+        rows = lanes((256, 512), 0) + 256 * i
+        to_slot[pl.ds(256 * i, 256), :] = jnp.where(rows == target, 1.0, 0.0).astype(BF16)
+    for i in range(2):
+        table = jnp.where(lanes((256, 1024)) == down_rows + 4 * i, 1.0, 0.0)
+        from_slot[pl.ds(256 * i, 256), :] = table.astype(BF16)
+
+
+def paint(first, second, to_slot, ax, ay, az, spread, out, total, fracs, tz, tt):
     piece = lanes((16, 128)) // 32
+    for z in range(NZ):
+        total[z] = first[z] + SECOND_ORDER * second[z]
     for axis in range(3):
-
-        @pl.loop(0, NZ)
-        def _(z, axis=axis):
-            def total(k):
-                return first[k] + SECOND_ORDER * second[k]
-
+        for z in range(NZ):
             if axis == 2:
-                slope = total((z + 1) % 16) - total((z + 15) % 16)
+                slope = total[(z + 1) % 16, 0:32, :] - total[(z + 15) % 16, 0:32, :]
+            elif axis == 1:
+                here = total[z, 0:32, :]
+                slope = up(here, 1) - down(here, 1)
             else:
-                here = total(z)
-                slope = up(here, axis) - down(here, axis)
-            value = 0.5 - 0.5 * slope
-            value = roll(roll(value, -2, 0)[0:32], -2, 1)
-            tz[pl.ds(z, 32, stride=16), :] = value
-
+                here = total[z]
+                slope = (up(here, 0) - down(here, 0))[0:32]
+            tz[pl.ds(z, 32, stride=16), :] = 0.5 - 0.5 * slope
         for q in range(4):
             tt[q] = jnp.transpose(tz[pl.ds(128 * q, 128), :])[0:64]
         for q in range(4):
@@ -450,8 +475,6 @@
                 for v in range(1, 4):
                     block = jnp.where(piece == v, roll(quarter[v], 32 * (v - k), 1), block)
                 fracs[axis, pl.ds(16 * (4 * q + k), 16), :] = block
-    for axis in range(3):
-        fracs[axis] = barrel(fracs[axis], az)
     fx, fy, fz = fracs[0], fracs[1], fracs[2]
     fields = []
     for wx in (1.0 - fx, fx):
@@ -460,16 +483,24 @@
             upper = q * fz
             fields.append(q - upper + group_roll(upper, 1))
     box = exact_right(jnp.concatenate(fields, axis=1), spread[...])
-    lane = lanes((256, 256))
-    box = jnp.where(lane == 240, ax.astype(F32), box)
-    box = jnp.where(lane == 241, ay.astype(F32), box)
-    target = jnp.concatenate([along, along + 4], axis=1)
-    table = jnp.where(lanes((1024, 512), 0) == target, 1.0, 0.0).astype(BF16)
-    stacked = jnp.concatenate([box[:, :128], box[:, 128:]], axis=0)
-    out[...] = exact_left(table, stacked).reshape(128, 8, 128)
-
-
-def own_cells(nbar, bias, arrived, counts, density, back, dens, pulls):
+    box_0, box_1 = barrel(box[:, :128], az), barrel(box[:, 128:], az)
+    lane = lanes((256, 128))
+    box_1 = jnp.where(lane == 112, ax.astype(F32), box_1)
+    box_1 = jnp.where(lane == 113, ay.astype(F32), box_1)
+    stacked = jnp.concatenate([box_0, box_1], axis=0)
+    out[...] = exact_left(to_slot[...], stacked).reshape(128, 8, 128)
+
+
+def weigh_counts(bias, counts, weighted):
+    for j in range(8):
+        value = None
+        for b in range(NBIN):
+            term = bias[b] * counts[b, :, pl.ds(128 * j, 128)].astype(F32)
+            value = term if value is None else value + term
+        weighted[pl.ds(32 * j, 32), :] = value
+
+
+def own_cells(nbar, bias, arrived, weighted, density, back, dens, pulls):
     data = arrived[...].reshape(1024, 128)
     second = lanes((1024, 128), 0) // 4 % 2
     is_second = second == 1
@@ -513,11 +544,9 @@
         here = dens[pl.ds(32 * j, 32), :]
         density[:, pl.ds(128 * j, 128)] = here
         contrast = here - 1.0
-        pull = jnp.zeros((32, 128), F32)
+        pull = weighted[pl.ds(32 * j, 32), :]
         for b in range(NBIN):
-            rate = nbar[b] * jnp.exp(bias[b] * contrast)
-            number = counts[b, :, pl.ds(128 * j, 128)].astype(F32)
-            pull = pull + bias[b] * (number - rate)
+            pull = pull - (bias[b] * nbar[b]) * jnp.exp(bias[b] * contrast)
         pulls[pl.ds(32 * j, 32), :] = pull
     pull = pulls[...]
     ahead = jnp.where(lanes((256, 128), 0) < 224, roll(pull, -32, 0), 0.0)
@@ -534,11 +563,10 @@
     back[...] = value.reshape(128, 8, 128)
 
 
-def forces(returned, place, az, spread_t, fracs, fx_out, fy_out, fz_out):
-    target = jnp.concatenate([place, place + 4], axis=0)
-    table = jnp.where(lanes((512, 1024)) == target, 1.0, 0.0).astype(BF16)
-    t = exact_left(table, returned[...].reshape(1024, 128))
-    box = jnp.concatenate([t[:256], t[256:]], axis=1)
+def forces(returned, from_slot, az, spread_t, fracs, fx_out, fy_out, fz_out):
+    t = exact_left(from_slot[...], returned[...].reshape(1024, 128))
+    amount = (16 - az) & 15
+    box = jnp.concatenate([barrel(t[:256], amount), barrel(t[256:], amount)], axis=1)
     corner = exact_right(box, spread_t[...])
     fx, fy, fz = fracs[0], fracs[1], fracs[2]
     along, across = [], []
@@ -547,7 +575,6 @@
         change = group_roll(here, 15) - here
         along.append(here + fz * change)
         across.append(change)
-    amount = (16 - az) & 15
     force_x = (1.0 - fy) * (along[2] - along[0]) + fy * (along[3] - along[1])
     force_y = (1.0 - fx) * (along[1] - along[0]) + fx * (along[3] - along[2])
     force_z = (1.0 - fx) * ((1.0 - fy) * across[0] + fy * across[1]) + fx * (
@@ -555,7 +582,6 @@
     )
     piece = lanes((16, 128)) // 32
     for force, out in ((force_x, fx_out), (force_y, fy_out), (force_z, fz_out)):
-        force = barrel(force, amount)
         for q in range(4):
             group = [force[16 * (4 * q + k) : 16 * (4 * q + k) + 16] for k in range(4)]
             for v in range(4):
@@ -600,35 +626,41 @@
         )
 
 
-def weights(first, pulled, out, part, wzz, wxz, wyz):
-    @pl.loop(0, NZ)
-    def _(z):
-        xx, yy, zz, xy, xz, yz = curvatures(
-            first[(z + 15) % 16], first[z], first[(z + 1) % 16]
-        )
+def weights(kept, pulled, out, wzz, wxz, wyz):
+    for z in range(NZ):
         g = pulled[z]
-        wx, wy = g * (yy + zz), g * (xx + zz)
-        wxy = -2.0 * g * xy
-        diff = up(wxy, 0) - down(wxy, 0)
-        part[z] = (
-            (up(wx, 0) - 2.0 * wx + down(wx, 0))
-            + (up(wy, 1) - 2.0 * wy + down(wy, 1))
-            + (up(diff, 1) - down(diff, 1)) * 0.25
-        )
-        wzz[z] = g * (xx + yy)
-        wxz[z] = -2.0 * g * xz
-        wyz[z] = -2.0 * g * yz
-
-    @pl.loop(0, NZ)
-    def _(z):
+        wzz[z] = g * kept[2, z]
+        wxz[z] = g * kept[4, z]
+        wyz[z] = g * kept[5, z]
+    for z in range(NZ):
         a, b = (z + 1) % 16, (z + 15) % 16
-        dx, dy = wxz[a] - wxz[b], wyz[a] - wyz[b]
-        out[z] = pack(
-            part[z]
-            + (wzz[a] - 2.0 * wzz[z] + wzz[b])
-            + (up(dx, 0) - down(dx, 0)) * 0.25
-            + (up(dy, 1) - down(dy, 1)) * 0.25
-        )
+        g = pulled[z]
+        wx, wy, wxy = g * kept[0, z], g * kept[1, z], g * kept[3, z]
+        dx = 0.25 * (wxz[a] - wxz[b])
+        dy = 0.25 * ((wyz[a] - wyz[b]) + (up(wxy, 0) - down(wxy, 0)))
+        along_x = up(wx + dx, 0) + down(wx - dx, 0)
+        along_y = up(wy + dy, 1) + down(wy - dy, 1)
+        along_z = wzz[a] + wzz[b]
+        out[z] = pack(along_x + along_y + along_z - 2.0 * (wx + wy + wzz[z]))
+
+
+def finish(pulled_modes, last_modes, sums, tzh, tzl, gradient):
+    slot = lanes((32, 128)) // 16
+    for m in range(16):
+        sums[m, 0:32, :] = pulled_modes[m, 0:32, :] * (1.0 / SECOND_ORDER) + last_modes[m, 0:32, :]
+    quarters = []
+    for q in range(4):
+        parts = []
+        for p in range(2):
+            value = None
+            for k in range(8):
+                piece = roll(sums[8 * p + k, 0:32, :], 16 * (k - q), 1)
+                value = piece if value is None else jnp.where(slot == k, piece, value)
+            parts.append(value)
+        quarters.append(jnp.concatenate(parts, axis=1))
+    t = right_product(jnp.concatenate(quarters, axis=0), tzh[...], tzl[...])
+    for q in range(4):
+        gradient[:, pl.ds(256 * q, 256)] = t[32 * q : 32 * q + 32]
 
 
 def columns(rows):
@@ -637,7 +669,7 @@
     return [turned[:, i : i + 1].astype(jnp.int32) for i in range(len(rows))]
 
 
-N_TABLES = 12
+N_TABLES = 14
 
 
 def whole_kernel(nbar, bias, delta, owner, anchor_x, anchor_y, anchor_z, *refs):
@@ -651,9 +683,10 @@
 
     held, (counts,) = take(N_TABLES), take(1)
     buffers = [take(8) for _ in range(4)]
-    first, second, pulled, last, part, wzz, wxz, wyz = take(8)
+    first, second, pulled, total, wzz, wxz, wyz, kept = take(8)
     src, factor, fracs, tz, tt = take(5)
-    payload, arrived, back, returned, dens, pulls = take(6)
+    payload, arrived, back, returned, dens, pulls, weighted = take(7)
+    to_slot, from_slot = take(2)
     fx, fy, fz, x_low, x_high, y_low, y_high = take(7)
     table_sem, *exchange_sems, own, hand_sem, edge_sem = rest
     row, col = lax.axis_index("row"), lax.axis_index("col")
@@ -681,44 +714,50 @@
     ]
     for load in loads:
         load.start()
-    tzh, tzl, *main, spread, spread_t = held
+    tzh, tzl, *main, spread, spread_t, bzh, bzl = held
     loads[0].wait()
     loads[1].wait()
     delta_modes(delta, tzh, tzl, buffers[0][0])
     pl.semaphore_wait(barrier, 127)
 
-    def ready():
+    owner_row = owner[...]
+    owner_col, ax, ay, az = columns((owner_row, anchor_x[...], anchor_y[...], anchor_z[...]))
+
+    def get_ready():
         factor[...] = modes_factor(row, col)
         for load in loads[2:]:
             load.wait()
 
     place = (row, col)
-    solve(place, buffers[0], semaphores(0), main, factor, first, pending, ready)
+    fill = (
+        get_ready,
+        lambda: weigh_counts(bias, counts, weighted),
+        lambda: place_tables(*slots(owner_row, owner_col), to_slot, from_slot),
+        None,
+    )
+    solve(place, buffers[0], semaphores(0), main, factor, first, pending, fill)
     source(first, src)
     to_modes(src, buffers[1][0])
-    solve(place, buffers[1], semaphores(1), main, factor, second, pending)
-    owner_row = owner[...]
-    rows = (owner_row, anchor_x[...], anchor_y[...], anchor_z[...])
-    owner_col, ax, ay, az = columns(rows)
-    along, down_rows = slots(owner_row, owner_col)
-    paint(first, second, along, ax, ay, az, spread, payload, fracs, tz, tt)
+    fill = (
+        lambda: keep_curvatures(first, kept, range(8)),
+        None,
+        None,
+        lambda: keep_curvatures(first, kept, range(8, 16)),
+    )
+    solve(place, buffers[1], semaphores(1), main, factor, second, pending, fill)
+    paint(first, second, to_slot, ax, ay, az, spread, payload, total, fracs, tz, tt)
     pending.append(handover(row, col, payload, arrived, hand_sem.at[0], hand_sem.at[1], hand_sem.at[2]))
-    own_cells(nbar, bias, arrived, counts, density, back, dens, pulls)
+    own_cells(nbar, bias, arrived, weighted, density, back, dens, pulls)
     pending.append(handover(row, col, back, returned, hand_sem.at[3], hand_sem.at[4], hand_sem.at[5]))
-    forces(returned, down_rows, az, spread_t, fracs, fx, fy, fz)
+    forces(returned, from_slot, az, spread_t, fracs, fx, fy, fz)
     neighbours(row, col, fx, fy, x_low, x_high, y_low, y_high, edge_sem, pending)
     divergence(fx, fy, fz, x_low, x_high, y_low, y_high, src, tz)
     to_modes(src, buffers[2][0])
     solve(place, buffers[2], semaphores(2), main, factor, pulled, pending)
-    weights(first, pulled, src, part, wzz, wxz, wyz)
+    weights(kept, pulled, src, wzz, wxz, wyz)
     to_modes(src, buffers[3][0])
-    solve(place, buffers[3], semaphores(3), main, factor, last, pending)
-
-    @pl.loop(0, NZ)
-    def _(z):
-        value = pulled[z] * (1.0 / SECOND_ORDER) + last[z]
-        gradient[z] = roll(roll(value, -2, 0)[0:32], -2, 1)
-
+    solve(place, buffers[3], semaphores(3), main, factor, None, pending)
+    finish(buffers[2][7], buffers[3][7], total, bzh, bzl, gradient)
     for copy in pending:
         copy.wait_send()
 
@@ -727,7 +766,7 @@
     t = np.zeros((16, 16, 16, 16))
     for y in range(16):
         t[y, :, :, y] = ZB.T
-    return two_terms(t.reshape(256, 256))
+    return t.reshape(256, 256)
 
 
 def spread_tables():
@@ -735,7 +774,12 @@
     return [spread.astype(jnp.bfloat16), spread.T.copy().astype(jnp.bfloat16)]
 
 
-TABLES = [*delta_table(), *make_tables(), *spread_tables()]
+TABLES = [
+    *two_terms(delta_table()),
+    *make_tables(),
+    *spread_tables(),
+    *two_terms(delta_table().T.copy()),
+]
 
 
 def on_device(delta, counts, nbar, bias, owner, anchor_x, anchor_y, anchor_z):
@@ -747,11 +791,12 @@
     for _ in range(4):
         for s in ((NROW, 16, 128), (NCOL, 32, 128), (NCOL, 64, 128), (NROW, XH, 128)):
             scratch += [pltpu.VMEM(s, F32), pltpu.VMEM(s, F32)]
-    scratch += [field] * 8
+    scratch += [field] * 7 + [pltpu.VMEM((6, NZ, XH, 128), F32)]
     scratch += [pltpu.VMEM((NZ, 16, 128), F32), pltpu.VMEM((64, GRID), F32)]
     scratch += [pltpu.VMEM((3, 256, 128), F32), pltpu.VMEM((512, 128), F32)]
     scratch += [pltpu.VMEM((4, 64, 128), F32)]
-    scratch += [hand] * 4 + [pltpu.VMEM((256, 128), F32)] * 2
+    scratch += [hand] * 4 + [pltpu.VMEM((256, 128), F32)] * 3
+    scratch += [pltpu.VMEM((1024, 512), BF16), pltpu.VMEM((512, 1024), BF16)]
     scratch += [pltpu.VMEM((4, 64, 128), F32)] * 3
     scratch += [pltpu.VMEM((64, 128), F32)] * 2 + [pltpu.VMEM((4, 8, 128), F32)] * 2
     scratch += [pltpu.SemaphoreType.DMA((len(tables) + 1,))]
@@ -763,10 +808,10 @@
         pltpu.SemaphoreType.DMA((2, 4)),
     ]
     smem = pl.BlockSpec(memory_space=pltpu.SMEM)
-    gradient, density = pl.pallas_call(
+    return pl.pallas_call(
         whole_kernel,
         out_shape=[
-            jax.ShapeDtypeStruct((NZ, CX, 128), F32),
+            jax.ShapeDtypeStruct((CX, CY * NZ), F32),
             jax.ShapeDtypeStruct((CX, CY * NZ), F32),
         ],
         in_specs=[smem] * 2 + [VM] * 5 + [ANY] * (1 + len(tables)),
@@ -777,8 +822,6 @@
         ),
         name="whole",
     )(nbar, bias, delta, *flat, counts, *tables)
-    gradient = gradient[:, :, :CY].transpose(1, 2, 0).reshape(CX, CY * NZ)
-    return gradient, density
 
 
 def solution(mesh):

time: 164 us -> 147 us (0.90)
  Pallas kernels: 160 us -> 144 us
    pallas_call x1, Pallas kernels: 160 us -> 144 us  [on_device(): pl.pallas_call(whole_kernel, out_shape=[jax.ShapeDtypeStruct((CX, CY * NZ...]
where the time goes in v3:
time: 147 us
  Pallas kernels  144 us (98%)
  local copies, waits for them, and re-layouts  2.26 us (2%)
    pallas_call x1, Pallas kernels, on_device(): pl.pallas_call(whole_kernel, out_shape=[jax.ShapeDtypeStruct((CX, CY * NZ...  144 us

profile of v3, /device:TPU:1, one launch (start us, length us, event | category | flops | bytes accessed | tf_op | source)
XLA Modules:
  0.0 146.9 jit_solution(5320575968946732440)
XLA Ops:
  0.6 144.0 %whole.1 = (f32[32,1024]{1,0:T(8,128)}, f32[32,1024]{1,0:T(8,128)}) custom-call(f32[8]{0:T(128)} %nbar.1, f32[8]{0:T(128)} %bias.1, f32[32,1024]{1,0:T(8,128)} %delta.1, s32[1,256]{1,0:T(1,128)} %bitcast.4, s32[1,256]{1,0:T(1,128)} %bitcast.5, s32[1,256]{1,0:T(1,128)} %bitcast.6, s32[1,256]{1,0:T(1,128)} %bitcast.7, s32[8,32,1024]{2,1,0:T(8,128)} %refs_0_.1, ...), custom_call_target="tpu_custom_call" | custom-call | tf_op jit(solution)/shard_map/whole/pallas_call | solution.py:811
  144.6 0.0 copy-start
  144.6 1.6 %copy.26 = f32[32,1024]{1,0:T(8,128)} copy(f32[32,1024]{1,0:T(8,128)} %get-tuple-element.4) | data formatting | bytes 262144
  146.2 0.0 copy-done
  146.2 0.7 copy.27
Async XLA Ops:
  144.6 1.6 %copy-start = (f32[32,1024]{1,0:T(8,128)S(1)}, f32[32,1024]{1,0:T(8,128)}, u32[]{:S(2)}) copy-start(f32[32,1024]{1,0:T(8,128)} %get-tuple-element.5) | copy-start | bytes 393220

commit v4 on v3

--- a/solution.py
+++ b/solution.py
@@ -47,7 +47,7 @@
     first, second = 32 * r + i, 32 * r + 16 + i
     c, k = np.divmod(np.arange(256), 32)
     low, high = 64 * c + k, 64 * c + 32 + k
-    fx = np.concatenate(
+    fx = np.stack(
         [
             basis[low][:, first],
             basis[high][:, second],
@@ -55,6 +55,7 @@
             basis[low][:, second],
         ]
     )
+    fx = fx.reshape(4, 4, 64, 256).transpose(1, 0, 2, 3).reshape(1024, 256)
     fy = basis.T
     gy = np.zeros((GRID, NCOL, 128))
     for c in range(NCOL):
@@ -108,13 +109,16 @@
     return high, middle, (rest - middle.astype(F32)).astype(BF16)
 
 
-def left_product(high, low, b):
-    n = b.shape[1]
+def left_product(high, low, pair, last):
+    n = last.shape[1]
+    t = dot(high, pair)
+    u = dot(low, pair)
+    return t[:, :n] + ((t[:, n:] + u[:, :n]) + (u[:, n:] + dot(high, last)))
+
+
+def left_terms(b):
     b0, b1, b2 = split_3(b)
-    pair = jnp.concatenate([b0, b1], axis=1)
-    t = dot(high, pair)
-    s = dot(low, pair)
-    return t[:, :n] + ((t[:, n:] + s[:, :n]) + (s[:, n:] + dot(high, b2)))
+    return jnp.concatenate([b0, b1], axis=1), b2
 
 
 def right_product(a, high, low):
@@ -189,45 +193,47 @@
     return out
 
 
-def distance(n, k):
-    around = lambda d: min(d, 4 - d)
-    return around(k % 4) + around(k // 4) if n == NROW else around(k // 2)
-
-
-def exchange(n, me, axis, src, dst, send, recv, own):
-    sends, recvs = [], []
-    for k in sorted(range(1, n), key=lambda k: -distance(n, k)):
-        peer = lax.rem(me + k, n)
-        origin = lax.rem(me + n - k, n)
-        copy = pltpu.make_async_remote_copy(
-            src_ref=src.at[peer],
-            dst_ref=dst.at[me],
-            send_sem=send.at[k],
-            recv_sem=recv.at[k],
-            device_id={axis: peer},
+class Exchange:
+    def __init__(self, n, me, axis, src, dst, send, recv, own, pending):
+        self.n, self.me, self.axis = n, me, axis
+        self.src, self.dst, self.send, self.recv, self.own = src, dst, send, recv, own
+        self.pending = pending
+
+    def copy(self, peer, slot):
+        return pltpu.make_async_remote_copy(
+            src_ref=self.src.at[peer],
+            dst_ref=self.dst.at[slot],
+            send_sem=self.send.at[peer],
+            recv_sem=self.recv.at[slot],
+            device_id={self.axis: peer},
             device_id_type=MESH,
         )
+
+    def start(self, peer):
+        copy = self.copy(peer, self.me)
         copy.start()
-        sends.append(copy)
-        recvs.append(
-            pltpu.make_async_remote_copy(
-                src_ref=src.at[peer],
-                dst_ref=dst.at[origin],
-                send_sem=send.at[k],
-                recv_sem=recv.at[k],
-                device_id={axis: peer},
-                device_id_type=MESH,
-            )
+        self.pending.append(copy)
+
+    def group(self, g, j, size):
+        if j:
+            for e in range(size):
+                self.start(g * size + e)
+            return
+        for e in range(1, size):
+            self.start(g * size + lax.rem(lax.rem(self.me, size) + e, size))
+        self.local = pltpu.make_async_copy(
+            self.src.at[self.me], self.dst.at[self.me], self.own
         )
-    copy = pltpu.make_async_copy(src.at[me], dst.at[me], own)
-    copy.start()
-    return sends, recvs, copy
-
-
-def arrive(state):
-    state[2].wait()
-    for copy in state[1]:
-        copy.wait_recv()
+        self.local.start()
+
+    def arrive(self):
+        self.local.wait()
+        for k in range(1, self.n):
+            origin = lax.rem(self.me + k, self.n)
+            self.copy(origin, origin).wait_recv()
+
+
+ORDER = (2, 1, 3, 0)
 
 
 def modes_factor(row, col):
@@ -246,20 +252,31 @@
     mo, r1, pk, r2, zb, r3, xb, r4 = buffers
     s1, q1, s2, q2, s3, q3, s4, q4, own = semaphores
     fxh, fxl, fyh, fyl, gyh, gyl, gxh, gxl = held
-    low_half = lanes((256, 128)) < 64
-    state1 = exchange(NROW, row, "row", mo, r1, s1, q1, own.at[0])
+    def groups(me, size):
+        return [(lax.rem(lax.div(me, size) + j, 4), j) for j in ORDER]
+
+    swap = Exchange(NROW, row, "row", mo, r1, s1, q1, own.at[0], pending)
+    for g, j in groups(row, 4):
+        swap.group(g, j, 4)
     if fill[0]:
         fill[0]()
-    arrive(state1)
-    t = left_product(fxh[...], fxl[...], r1[...].reshape(256, 128))
-    packed = jnp.where(low_half, t[:256], t[256:512]) + roll(
-        jnp.where(low_half, t[512:768], t[768:]), 64, 1
-    )
-    pk[...] = packed.reshape(NCOL, 32, 128)
-    state2 = exchange(NCOL, col, "col", pk, r2, s2, q2, own.at[1])
+    swap.arrive()
+
+    swap = Exchange(NCOL, col, "col", pk, r2, s2, q2, own.at[1], pending)
+    pair, last = left_terms(r1[...].reshape(256, 128))
+    low_half = lanes((64, 128)) < 64
+    for g, j in groups(col, 2):
+        rows = pl.ds(pl.multiple_of(256 * g, 256), 256)
+        t = left_product(fxh[rows, :], fxl[rows, :], pair, last)
+        packed = jnp.where(low_half, t[:64], t[64:128]) + roll(
+            jnp.where(low_half, t[128:192], t[192:]), 64, 1
+        )
+        pk[pl.ds(2 * g, 2)] = packed.reshape(2, 32, 128)
+        swap.group(g, j, 2)
     if fill[1]:
         fill[1]()
-    arrive(state2)
+    swap.arrive()
+
     half = lanes((32, 128)) < 64
     top, bottom = [], []
     for p in range(4):
@@ -270,24 +287,34 @@
         [jnp.concatenate(top, axis=1), jnp.concatenate(bottom, axis=1)], axis=0
     )
     modes = right_product(full, fyh[...], fyl[...]) * factor[...]
-    back = right_product(modes, gyh[...], gyl[...])
-    for c in range(NCOL):
-        zb[c] = back[:, 128 * c : 128 * (c + 1)]
-    state3 = exchange(NCOL, col, "col", zb, r3, s3, q3, own.at[2])
+    swap = Exchange(NCOL, col, "col", zb, r3, s3, q3, own.at[2], pending)
+    pair = jnp.concatenate(split_3(modes), axis=0)
+    for g, j in groups(col, 2):
+        lane = pl.ds(pl.multiple_of(256 * g, 256), 256)
+        t = dot(pair, gyh[:, lane])
+        u = dot(pair[:128], gyl[:, lane])
+        back = t[:64] + ((t[64:128] + u[:64]) + (u[64:] + t[128:]))
+        zb[2 * g] = back[:, :128]
+        zb[2 * g + 1] = back[:, 128:]
+        swap.group(g, j, 2)
     if fill[2]:
         fill[2]()
-    arrive(state3)
-    xb[...] = left_product(gxh[...], gxl[...], r3[...].reshape(GRID, 128)).reshape(NROW, XH, 128)
-    state4 = exchange(NROW, row, "row", xb, r4, s4, q4, own.at[3])
+    swap.arrive()
+
+    swap = Exchange(NROW, row, "row", xb, r4, s4, q4, own.at[3], pending)
+    pair, last = left_terms(r3[...].reshape(GRID, 128))
+    for g, j in groups(row, 4):
+        rows = pl.ds(pl.multiple_of(4 * XH * g, 4 * XH), 4 * XH)
+        t = left_product(gxh[rows, :], gxl[rows, :], pair, last)
+        xb[pl.ds(4 * g, 4)] = t.reshape(4, XH, 128)
+        swap.group(g, j, 4)
     if fill[3]:
         fill[3]()
-    arrive(state4)
+    swap.arrive()
     for s in range(5 if out is not None else 0):
         rows = pl.ds(8 * s, 8)
         for z, value in enumerate(inverse_z([r4[m, rows, :] for m in range(16)])):
             out[z, rows, :] = value
-    for state in (state1, state2, state3, state4):
-        pending.extend(state[0])
 
 
 def to_modes(src, mo):
@@ -316,34 +343,46 @@
         mo[m] = value
 
 
-def handover(row, col, src, dst, send, recv, own):
-    me = row * NCOL + col
-
-    @pl.loop(1, 128)
-    def _(k):
-        peer = lax.rem(me + k, 128)
-        pltpu.make_async_remote_copy(
-            src_ref=src.at[peer],
-            dst_ref=dst.at[me],
-            send_sem=send,
-            recv_sem=recv,
-            device_id={"row": peer // NCOL, "col": lax.rem(peer, NCOL)},
+class Handover:
+    def __init__(self, row, col, src, dst, sems):
+        self.me, self.col = row * NCOL + col, col
+        self.src, self.dst = src, dst
+        self.send, self.recv, self.own = sems
+
+    def groups(self):
+        return [(lax.rem(lax.div(self.me, 32) + j, 4), j) for j in ORDER]
+
+    def group(self, g, j):
+        @pl.loop(0 if j else 1, 32)
+        def _(k):
+            peer = 32 * g + lax.rem(lax.rem(self.me, 32) + k, 32)
+            pltpu.make_async_remote_copy(
+                src_ref=self.src.at[peer],
+                dst_ref=self.dst.at[self.me],
+                send_sem=self.send,
+                recv_sem=self.recv,
+                device_id={"row": lax.div(peer, NCOL), "col": lax.rem(peer, NCOL)},
+                device_id_type=MESH,
+            ).start()
+
+        if j == 0:
+            self.local = pltpu.make_async_copy(
+                self.src.at[self.me], self.dst.at[self.me], self.own
+            )
+            self.local.start()
+
+    def arrive(self, pending):
+        self.local.wait()
+        all_of_them = pltpu.make_async_remote_copy(
+            src_ref=self.src.at[pl.ds(0, 127)],
+            dst_ref=self.dst.at[pl.ds(0, 127)],
+            send_sem=self.send,
+            recv_sem=self.recv,
+            device_id={"col": lax.rem(self.col + 1, NCOL)},
             device_id_type=MESH,
-        ).start()
-
-    copy = pltpu.make_async_copy(src.at[me], dst.at[me], own)
-    copy.start()
-    copy.wait()
-    all_of_them = pltpu.make_async_remote_copy(
-        src_ref=src.at[pl.ds(0, 127)],
-        dst_ref=dst.at[pl.ds(0, 127)],
-        send_sem=send,
-        recv_sem=recv,
-        device_id={"col": lax.rem(col + 1, NCOL)},
-        device_id_type=MESH,
-    )
-    all_of_them.wait_recv()
-    return all_of_them
+        )
+        all_of_them.wait_recv()
+        pending.append(all_of_them)
 
 
 def neighbours(row, col, fx, fy, x_low, x_high, y_low, y_high, sems, pending):
@@ -451,7 +490,7 @@
         from_slot[pl.ds(256 * i, 256), :] = table.astype(BF16)
 
 
-def paint(first, second, to_slot, ax, ay, az, spread, out, total, fracs, tz, tt):
+def paint(first, second, to_slot, ax, ay, az, spread, out, total, fracs, tz, tt, hand):
     piece = lanes((16, 128)) // 32
     for z in range(NZ):
         total[z] = first[z] + SECOND_ORDER * second[z]
@@ -488,7 +527,11 @@
     box_1 = jnp.where(lane == 112, ax.astype(F32), box_1)
     box_1 = jnp.where(lane == 113, ay.astype(F32), box_1)
     stacked = jnp.concatenate([box_0, box_1], axis=0)
-    out[...] = exact_left(to_slot[...], stacked).reshape(128, 8, 128)
+    pair = jnp.concatenate(split(stacked), axis=1)
+    for g, j in hand.groups():
+        t = dot(to_slot[pl.ds(pl.multiple_of(256 * g, 256), 256), :], pair)
+        out[pl.ds(32 * g, 32)] = (t[:, :128] + t[:, 128:]).reshape(32, 8, 128)
+        hand.group(g, j)
 
 
 def weigh_counts(bias, counts, weighted):
@@ -500,16 +543,28 @@
         weighted[pl.ds(32 * j, 32), :] = value
 
 
-def own_cells(nbar, bias, arrived, weighted, density, back, dens, pulls):
+def geometry(data):
+    n = data.shape[0]
+    second = lanes((n, 128), 0) // 4 % 2
+
+    def both(lane):
+        column = jnp.broadcast_to(data[:, lane : lane + 1], (n, 128))
+        return jnp.where(second == 1, column, roll(column, -4, 0)).astype(jnp.int32)
+
+    ax, ay = both(112), both(113)
+    step = ay & 7
+    return (
+        second,
+        (ay >> 3) * 32 + ax,
+        step,
+        (3 * second + 3 + ay) & 7,
+        lanes((n, 128)) >= step * 16,
+    )
+
+
+def own_cells(nbar, bias, arrived, weighted, density, back, dens, pulls, hand):
     data = arrived[...].reshape(1024, 128)
-    second = lanes((1024, 128), 0) // 4 % 2
-    is_second = second == 1
-
-    def both(lane):
-        column = jnp.broadcast_to(data[:, lane : lane + 1], (1024, 128))
-        return jnp.where(is_second, column, roll(column, -4, 0)).astype(jnp.int32)
-
-    ax, ay = both(112), both(113)
+    second, base, step, side_step, stay = geometry(data)
     flipped = jnp.concatenate(
         [jnp.transpose(data[128 * i : 128 * (i + 1)]) for i in range(8)], axis=1
     )
@@ -522,11 +577,7 @@
 
     ax_row, ay_row = both_row(112), both_row(113)
     base_row = (ay_row >> 3) * 32 + ax_row
-    base = (ay >> 3) * 32 + ax
     lane = lanes((1024, 128))
-    step = ay & 7
-    side_step = (3 * second + 3 + ay) & 7
-    stay = lane >= step * 16
     main = barrel_16(jnp.where(lane < 80, data, 0.0), step)
     side_mask = (lane >= 80) & (lane < 112 + 16 * (1 - second))
     side = barrel_16(jnp.where(side_mask, data, 0.0), side_step)
@@ -552,15 +603,20 @@
     ahead = jnp.where(lanes((256, 128), 0) < 224, roll(pull, -32, 0), 0.0)
     both_pulls = jnp.concatenate([*split(pull), *split(ahead)], axis=1)
 
-    def picked(offset, amount):
-        wide = jnp.concatenate([base + offset, base + offset], axis=1)
-        table = jnp.where(lanes((1024, 256)) == wide, 1.0, 0.0).astype(BF16)
-        t = dot(table, both_pulls)
-        value = jnp.where(stay, t[:, :128] + t[:, 128:256], t[:, 256:384] + t[:, 384:])
-        return barrel_16(value, (8 - amount) & 7)
-
-    value = jnp.where(lane < 80, picked(2 * second, step), picked(1, side_step))
-    back[...] = value.reshape(128, 8, 128)
+    lane = lanes((256, 128))
+    row_of = lanes((256, 256))
+    for g, j in hand.groups():
+        data = arrived[pl.ds(32 * g, 32)].reshape(256, 128)
+        second, base, step, side_step, stay = geometry(data)
+        parts = []
+        for offset, amount in ((2 * second, step), (1, side_step)):
+            wide = base + offset
+            table = jnp.where(row_of == jnp.concatenate([wide, wide], axis=1), 1.0, 0.0)
+            t = dot(table.astype(BF16), both_pulls)
+            value = jnp.where(stay, t[:, :128] + t[:, 128:256], t[:, 256:384] + t[:, 384:])
+            parts.append(barrel_16(value, (8 - amount) & 7))
+        back[pl.ds(32 * g, 32)] = jnp.where(lane < 80, *parts).reshape(32, 8, 128)
+        hand.group(g, j)
 
 
 def forces(returned, from_slot, az, spread_t, fracs, fx_out, fy_out, fz_out):
@@ -745,10 +801,12 @@
         lambda: keep_curvatures(first, kept, range(8, 16)),
     )
     solve(place, buffers[1], semaphores(1), main, factor, second, pending, fill)
-    paint(first, second, to_slot, ax, ay, az, spread, payload, total, fracs, tz, tt)
-    pending.append(handover(row, col, payload, arrived, hand_sem.at[0], hand_sem.at[1], hand_sem.at[2]))
-    own_cells(nbar, bias, arrived, weighted, density, back, dens, pulls)
-    pending.append(handover(row, col, back, returned, hand_sem.at[3], hand_sem.at[4], hand_sem.at[5]))
+    hand = Handover(row, col, payload, arrived, [hand_sem.at[i] for i in range(3)])
+    paint(first, second, to_slot, ax, ay, az, spread, payload, total, fracs, tz, tt, hand)
+    hand.arrive(pending)
+    hand = Handover(row, col, back, returned, [hand_sem.at[i] for i in range(3, 6)])
+    own_cells(nbar, bias, arrived, weighted, density, back, dens, pulls, hand)
+    hand.arrive(pending)
     forces(returned, from_slot, az, spread_t, fracs, fx, fy, fz)
     neighbours(row, col, fx, fy, x_low, x_high, y_low, y_high, edge_sem, pending)
     divergence(fx, fy, fz, x_low, x_high, y_low, y_high, src, tz)

time: 147 us -> 139 us (0.946)
  Pallas kernels: 144 us -> 136 us
    pallas_call x1, Pallas kernels: 144 us -> 136 us  [on_device(): pl.pallas_call(whole_kernel, out_shape=[jax.ShapeDtypeStruct((CX, CY * NZ...]
where the time goes in v4:
time: 139 us
  Pallas kernels  136 us (98%)
  local copies, waits for them, and re-layouts  2.26 us (2%)
    pallas_call x1, Pallas kernels, on_device(): pl.pallas_call(whole_kernel, out_shape=[jax.ShapeDtypeStruct((CX, CY * NZ...  136 us

profile of v4, /device:TPU:1, one launch (start us, length us, event | category | flops | bytes accessed | tf_op | source)
XLA Modules:
  0.0 139.1 jit_solution(3574578043217655568)
XLA Ops:
  0.6 136.2 %whole.1 = (f32[32,1024]{1,0:T(8,128)}, f32[32,1024]{1,0:T(8,128)}) custom-call(f32[8]{0:T(128)} %nbar.1, f32[8]{0:T(128)} %bias.1, f32[32,1024]{1,0:T(8,128)} %delta.1, s32[1,256]{1,0:T(1,128)} %bitcast.4, s32[1,256]{1,0:T(1,128)} %bitcast.5, s32[1,256]{1,0:T(1,128)} %bitcast.6, s32[1,256]{1,0:T(1,128)} %bitcast.7, s32[8,32,1024]{2,1,0:T(8,128)} %refs_0_.1, ...), custom_call_target="tpu_custom_call" | custom-call | tf_op jit(solution)/shard_map/whole/pallas_call | solution.py:869
  136.8 0.0 copy-start
  136.9 1.6 %copy.26 = f32[32,1024]{1,0:T(8,128)} copy(f32[32,1024]{1,0:T(8,128)} %get-tuple-element.4) | data formatting | bytes 262144
  138.5 0.0 copy-done
  138.5 0.7 copy.27
Async XLA Ops:
  136.8 1.6 %copy-start = (f32[32,1024]{1,0:T(8,128)S(1)}, f32[32,1024]{1,0:T(8,128)}, u32[]{:S(2)}) copy-start(f32[32,1024]{1,0:T(8,128)} %get-tuple-element.5) | copy-start | bytes 393220

commit v5 on v4

--- a/solution.py
+++ b/solution.py
@@ -56,6 +56,15 @@
         ]
     )
     fx = fx.reshape(4, 4, 64, 256).transpose(1, 0, 2, 3).reshape(1024, 256)
+    hx = np.stack(
+        [
+            basis[low][:, first].T,
+            basis[high][:, second].T,
+            basis[low][:, second].T,
+            basis[high][:, first].T,
+        ]
+    )
+    hx = hx.reshape(4, 4, 64, 256).transpose(1, 0, 2, 3).reshape(1024, 256)
     fy = basis.T
     gy = np.zeros((GRID, NCOL, 128))
     for c in range(NCOL):
@@ -66,7 +75,7 @@
         for x in range(-2, CX + 2):
             gx[r, x % XH] = basis[:, (CX * r + x) % GRID]
     tables = []
-    for t in (fx, fy, gy.reshape(GRID, NCOL * 128), gx.reshape(NROW * XH, GRID)):
+    for t in (fx, fy, gy.reshape(GRID, NCOL * 128), gx.reshape(NROW * XH, GRID), hx):
         tables.extend(two_terms(t))
     return tables
 
@@ -95,6 +104,10 @@
 
 def dot(a, b):
     return lax.dot_general(a, b, (((1,), (0,)), ((), ())), preferred_element_type=F32)
+
+
+def dot_turned(a, b):
+    return lax.dot_general(a, b, (((1,), (1,)), ((), ())), preferred_element_type=F32)
 
 
 def split(x):
@@ -251,7 +264,7 @@
     row, col = place
     mo, r1, pk, r2, zb, r3, xb, r4 = buffers
     s1, q1, s2, q2, s3, q3, s4, q4, own = semaphores
-    fxh, fxl, fyh, fyl, gyh, gyl, gxh, gxl = held
+    fxh, fxl, fyh, fyl, gyh, gyl, gxh, gxl, hxh, hxl = held
     def groups(me, size):
         return [(lax.rem(lax.div(me, size) + j, 4), j) for j in ORDER]
 
@@ -289,7 +302,16 @@
     modes = right_product(full, fyh[...], fyl[...]) * factor[...]
     swap = Exchange(NCOL, col, "col", zb, r3, s3, q3, own.at[2], pending)
     pair = jnp.concatenate(split_3(modes), axis=0)
-    for g, j in groups(col, 2):
+    for g, j in groups(col, 2) if out is None else ():
+        rows = pl.ds(pl.multiple_of(128 * g, 128), 128)
+        t = dot_turned(pair, fyh[rows, :])
+        u = dot_turned(pair[:128], fyl[rows, :])
+        back = t[:64] + ((t[64:128] + u[:64]) + (u[64:] + t[128:]))
+        a, b = back[:32], back[32:]
+        zb[2 * g] = jnp.where(half, a, roll(b, 64, 1))
+        zb[2 * g + 1] = jnp.where(half, roll(a, 64, 1), b)
+        swap.group(g, j, 2)
+    for g, j in groups(col, 2) if out is not None else ():
         lane = pl.ds(pl.multiple_of(256 * g, 256), 256)
         t = dot(pair, gyh[:, lane])
         u = dot(pair[:128], gyl[:, lane])
@@ -302,8 +324,16 @@
     swap.arrive()
 
     swap = Exchange(NROW, row, "row", xb, r4, s4, q4, own.at[3], pending)
-    pair, last = left_terms(r3[...].reshape(GRID, 128))
-    for g, j in groups(row, 4):
+    pair, last = left_terms(r3[...].reshape(-1, 128))
+    for g, j in groups(row, 4) if out is None else ():
+        rows = pl.ds(pl.multiple_of(256 * g, 256), 256)
+        t = left_product(hxh[rows, :], hxl[rows, :], pair, last)
+        packed = jnp.where(low_half, t[:64], t[64:128]) + roll(
+            jnp.where(low_half, t[128:192], t[192:]), 64, 1
+        )
+        xb[pl.ds(4 * g, 4)] = packed.reshape(4, 16, 128)
+        swap.group(g, j, 4)
+    for g, j in groups(row, 4) if out is not None else ():
         rows = pl.ds(pl.multiple_of(4 * XH * g, 4 * XH), 4 * XH)
         t = left_product(gxh[rows, :], gxl[rows, :], pair, last)
         xb[pl.ds(4 * g, 4)] = t.reshape(4, XH, 128)
@@ -385,30 +415,25 @@
         pending.append(all_of_them)
 
 
-def neighbours(row, col, fx, fy, x_low, x_high, y_low, y_high, sems, pending):
+def start_edges(row, col, axis, field, low, high, sems):
+    if axis == 0:
+        n, me, name, last, first = NROW, row, "row", field.at[3], field.at[0]
+    else:
+        n, me, name = NCOL, col, "col"
+        last, first = field.at[:, pl.ds(56, 8)], field.at[:, pl.ds(0, 8)]
     copies = []
-    for i, (axis, peer, src, dst) in enumerate(
-        (
-            ("row", lax.rem(row + 1, NROW), fx.at[3], x_low),
-            ("row", lax.rem(row + NROW - 1, NROW), fx.at[0], x_high),
-            ("col", lax.rem(col + 1, NCOL), fy.at[:, pl.ds(56, 8)], y_low),
-            ("col", lax.rem(col + NCOL - 1, NCOL), fy.at[:, pl.ds(0, 8)], y_high),
+    for i, (step, src, dst) in enumerate(((1, last, low), (n - 1, first, high))):
+        copy = pltpu.make_async_remote_copy(
+            src_ref=src,
+            dst_ref=dst,
+            send_sem=sems.at[0, 2 * axis + i],
+            recv_sem=sems.at[1, 2 * axis + i],
+            device_id={name: lax.rem(me + step, n)},
+            device_id_type=MESH,
         )
-    ):
-        copies.append(
-            pltpu.make_async_remote_copy(
-                src_ref=src,
-                dst_ref=dst,
-                send_sem=sems.at[0, i],
-                recv_sem=sems.at[1, i],
-                device_id={axis: peer},
-                device_id_type=MESH,
-            )
-        )
-        copies[-1].start()
-    for copy in copies:
-        copy.wait_recv()
-    pending.extend(copies)
+        copy.start()
+        copies.append(copy)
+    return copies
 
 
 VM = pl.BlockSpec(memory_space=pltpu.VMEM)
@@ -619,7 +644,7 @@
         hand.group(g, j)
 
 
-def forces(returned, from_slot, az, spread_t, fracs, fx_out, fy_out, fz_out):
+def forces(returned, from_slot, az, spread_t, fracs, outs, after):
     t = exact_left(from_slot[...], returned[...].reshape(1024, 128))
     amount = (16 - az) & 15
     box = jnp.concatenate([barrel(t[:256], amount), barrel(t[256:], amount)], axis=1)
@@ -637,7 +662,7 @@
         (1.0 - fy) * across[2] + fy * across[3]
     )
     piece = lanes((16, 128)) // 32
-    for force, out in ((force_x, fx_out), (force_y, fy_out), (force_z, fz_out)):
+    for axis, (force, out) in enumerate(zip((force_x, force_y, force_z), outs)):
         for q in range(4):
             group = [force[16 * (4 * q + k) : 16 * (4 * q + k) + 16] for k in range(4)]
             for v in range(4):
@@ -645,6 +670,7 @@
                 for k in range(1, 4):
                     value = jnp.where(piece == k, roll(group[k], 32 * (k - v), 1), value)
                 out[q, pl.ds(v, 16, stride=4), :] = value
+        after[axis]()
 
 
 def divergence(fx, fy, fz, x_low, x_high, y_low, y_high, out, tz):
@@ -703,7 +729,9 @@
 def finish(pulled_modes, last_modes, sums, tzh, tzl, gradient):
     slot = lanes((32, 128)) // 16
     for m in range(16):
-        sums[m, 0:32, :] = pulled_modes[m, 0:32, :] * (1.0 / SECOND_ORDER) + last_modes[m, 0:32, :]
+        here = last_modes[m]
+        whole = jnp.concatenate([here, roll(here, 64, 1)], axis=0)
+        sums[m, 0:32, :] = pulled_modes[m, 0:32, :] * (1.0 / SECOND_ORDER) + whole
     quarters = []
     for q in range(4):
         parts = []
@@ -725,7 +753,7 @@
     return [turned[:, i : i + 1].astype(jnp.int32) for i in range(len(rows))]
 
 
-N_TABLES = 14
+N_TABLES = 16
 
 
 def whole_kernel(nbar, bias, delta, owner, anchor_x, anchor_y, anchor_z, *refs):
@@ -768,35 +796,39 @@
         pltpu.make_async_copy(t, h, table_sem.at[i])
         for i, (t, h) in enumerate(zip((*tables, counts_far), (*held, counts)))
     ]
-    for load in loads:
+    for load in loads[:4]:
         load.start()
     tzh, tzl, *main, spread, spread_t, bzh, bzl = held
     loads[0].wait()
     loads[1].wait()
     delta_modes(delta, tzh, tzl, buffers[0][0])
+    for load in loads[4:]:
+        load.start()
     pl.semaphore_wait(barrier, 127)
 
     owner_row = owner[...]
     owner_col, ax, ay, az = columns((owner_row, anchor_x[...], anchor_y[...], anchor_z[...]))
 
-    def get_ready():
+    def loaded(first_load, end):
+        for load in loads[first_load:end]:
+            load.wait()
+
+    def fill_0():
         factor[...] = modes_factor(row, col)
-        for load in loads[2:]:
-            load.wait()
+        loaded(2, 4)
+
+    def fill_2():
+        place_tables(*slots(owner_row, owner_col), to_slot, from_slot)
+        loaded(8, 10)
 
     place = (row, col)
-    fill = (
-        get_ready,
-        lambda: weigh_counts(bias, counts, weighted),
-        lambda: place_tables(*slots(owner_row, owner_col), to_slot, from_slot),
-        None,
-    )
+    fill = (fill_0, lambda: loaded(4, 8), fill_2, lambda: loaded(10, None))
     solve(place, buffers[0], semaphores(0), main, factor, first, pending, fill)
     source(first, src)
     to_modes(src, buffers[1][0])
     fill = (
         lambda: keep_curvatures(first, kept, range(8)),
-        None,
+        lambda: weigh_counts(bias, counts, weighted),
         None,
         lambda: keep_curvatures(first, kept, range(8, 16)),
     )
@@ -807,8 +839,16 @@
     hand = Handover(row, col, back, returned, [hand_sem.at[i] for i in range(3, 6)])
     own_cells(nbar, bias, arrived, weighted, density, back, dens, pulls, hand)
     hand.arrive(pending)
-    forces(returned, from_slot, az, spread_t, fracs, fx, fy, fz)
-    neighbours(row, col, fx, fy, x_low, x_high, y_low, y_high, edge_sem, pending)
+    edges = []
+    after = (
+        lambda: edges.extend(start_edges(row, col, 0, fx, x_low, x_high, edge_sem)),
+        lambda: edges.extend(start_edges(row, col, 1, fy, y_low, y_high, edge_sem)),
+        lambda: None,
+    )
+    forces(returned, from_slot, az, spread_t, fracs, (fx, fy, fz), after)
+    for copy in edges:
+        copy.wait_recv()
+    pending.extend(edges)
     divergence(fx, fy, fz, x_low, x_high, y_low, y_high, src, tz)
     to_modes(src, buffers[2][0])
     solve(place, buffers[2], semaphores(2), main, factor, pulled, pending)
@@ -846,8 +886,9 @@
     field = pltpu.VMEM((NZ, XH, 128), F32)
     hand = pltpu.VMEM((128, 8, 128), F32)
     scratch = [pltpu.VMEM(t.shape, BF16) for t in tables] + [pltpu.VMEM(counts.shape, jnp.int32)]
-    for _ in range(4):
-        for s in ((NROW, 16, 128), (NCOL, 32, 128), (NCOL, 64, 128), (NROW, XH, 128)):
+    for i in range(4):
+        deep, tall = (64, XH) if i < 3 else (32, 16)
+        for s in ((NROW, 16, 128), (NCOL, 32, 128), (NCOL, deep, 128), (NROW, tall, 128)):
             scratch += [pltpu.VMEM(s, F32), pltpu.VMEM(s, F32)]
     scratch += [field] * 7 + [pltpu.VMEM((6, NZ, XH, 128), F32)]
     scratch += [pltpu.VMEM((NZ, 16, 128), F32), pltpu.VMEM((64, GRID), F32)]

time: 139 us -> 137 us (0.986)
  Pallas kernels: 136 us -> 133 us
    pallas_call x1, Pallas kernels: 136 us -> 133 us  [on_device(): pl.pallas_call(whole_kernel, out_shape=[jax.ShapeDtypeStruct((CX, CY * NZ...]
where the time goes in v5:
time: 137 us; the launch traced here: 136 us
  Pallas kernels  133 us (97%)
  local copies, waits for them, and re-layouts  2.26 us (2%)
    pallas_call x1, Pallas kernels, on_device(): pl.pallas_call(whole_kernel, out_shape=[jax.ShapeDtypeStruct((CX, CY * NZ...  133 us

profile of v5, /device:TPU:1, one launch (start us, length us, event | category | flops | bytes accessed | tf_op | source)
XLA Modules:
  0.0 136.4 jit_solution(3525423028105207941)
XLA Ops:
  0.6 133.4 %whole.1 = (f32[32,1024]{1,0:T(8,128)}, f32[32,1024]{1,0:T(8,128)}) custom-call(f32[8]{0:T(128)} %nbar.1, f32[8]{0:T(128)} %bias.1, f32[32,1024]{1,0:T(8,128)} %delta.1, s32[1,256]{1,0:T(1,128)} %bitcast.4, s32[1,256]{1,0:T(1,128)} %bitcast.5, s32[1,256]{1,0:T(1,128)} %bitcast.6, s32[1,256]{1,0:T(1,128)} %bitcast.7, s32[8,32,1024]{2,1,0:T(8,128)} %refs_0_.1, ...), custom_call_target="tpu_custom_call" | custom-call | tf_op jit(solution)/shard_map/whole/pallas_call | solution.py:910
  134.1 0.0 copy-start
  134.1 1.6 %copy.28 = f32[32,1024]{1,0:T(8,128)} copy(f32[32,1024]{1,0:T(8,128)} %get-tuple-element.4) | data formatting | bytes 262144
  135.7 0.0 copy-done
  135.7 0.7 copy.29
Async XLA Ops:
  134.1 1.6 %copy-start = (f32[32,1024]{1,0:T(8,128)S(1)}, f32[32,1024]{1,0:T(8,128)}, u32[]{:S(2)}) copy-start(f32[32,1024]{1,0:T(8,128)} %get-tuple-element.5) | copy-start | bytes 393220

commit v6 on v5

--- a/solution.py
+++ b/solution.py
@@ -782,15 +782,14 @@
 
     barrier = pltpu.get_barrier_semaphore()
 
-    @pl.loop(1, 128)
-    def _(k):
-        peer = lax.rem(me + k, 128)
-        pl.semaphore_signal(
-            barrier,
-            inc=1,
-            device_id={"row": peer // NCOL, "col": lax.rem(peer, NCOL)},
-            device_id_type=MESH,
-        )
+    for n, here, axis in ((NROW, row, "row"), (NCOL, col, "col")):
+        for k in range(1, n):
+            pl.semaphore_signal(
+                barrier,
+                inc=1,
+                device_id={axis: lax.rem(here + k, n)},
+                device_id_type=MESH,
+            )
 
     loads = [
         pltpu.make_async_copy(t, h, table_sem.at[i])
@@ -804,7 +803,7 @@
     delta_modes(delta, tzh, tzl, buffers[0][0])
     for load in loads[4:]:
         load.start()
-    pl.semaphore_wait(barrier, 127)
+    pl.semaphore_wait(barrier, NROW + NCOL - 2)
 
     owner_row = owner[...]
     owner_col, ax, ay, az = columns((owner_row, anchor_x[...], anchor_y[...], anchor_z[...]))

time: 137 us -> 134 us (0.978)
  Pallas kernels: 133 us -> 131 us
    pallas_call x1, Pallas kernels: 133 us -> 131 us  [on_device(): pl.pallas_call(whole_kernel, out_shape=[jax.ShapeDtypeStruct((CX, CY * NZ...]
where the time goes in v6:
time: 134 us
  Pallas kernels  131 us (98%)
  local copies, waits for them, and re-layouts  2.26 us (2%)
    pallas_call x1, Pallas kernels, on_device(): pl.pallas_call(whole_kernel, out_shape=[jax.ShapeDtypeStruct((CX, CY * NZ...  131 us

profile of v6, /device:TPU:1, one launch (start us, length us, event | category | flops | bytes accessed | tf_op | source)
XLA Modules:
  0.0 133.7 jit_solution(6288984813310064509)
XLA Ops:
  0.6 130.8 %whole.1 = (f32[32,1024]{1,0:T(8,128)}, f32[32,1024]{1,0:T(8,128)}) custom-call(f32[8]{0:T(128)} %nbar.1, f32[8]{0:T(128)} %bias.1, f32[32,1024]{1,0:T(8,128)} %delta.1, s32[1,256]{1,0:T(1,128)} %bitcast.4, s32[1,256]{1,0:T(1,128)} %bitcast.5, s32[1,256]{1,0:T(1,128)} %bitcast.6, s32[1,256]{1,0:T(1,128)} %bitcast.7, s32[8,32,1024]{2,1,0:T(8,128)} %refs_0_.1, ...), custom_call_target="tpu_custom_call" | custom-call | tf_op jit(solution)/shard_map/whole/pallas_call | solution.py:909
  131.4 0.0 copy-start
  131.4 1.6 %copy.28 = f32[32,1024]{1,0:T(8,128)} copy(f32[32,1024]{1,0:T(8,128)} %get-tuple-element.4) | data formatting | bytes 262144
  133.0 0.0 copy-done
  133.0 0.7 copy.29
Async XLA Ops:
  131.4 1.6 %copy-start = (f32[32,1024]{1,0:T(8,128)S(1)}, f32[32,1024]{1,0:T(8,128)}, u32[]{:S(2)}) copy-start(f32[32,1024]{1,0:T(8,128)} %get-tuple-element.5) | copy-start | bytes 393220

commit v7 on v6

--- a/solution.py
+++ b/solution.py
@@ -123,9 +123,10 @@
 
 
 def left_product(high, low, pair, last):
-    n = last.shape[1]
-    t = dot(high, pair)
-    u = dot(low, pair)
+    m, n = high.shape[0], last.shape[1]
+    t = dot(jnp.concatenate([high, low], axis=0), pair)
+    u = t[m:]
+    t = t[:m]
     return t[:, :n] + ((t[:, n:] + u[:, :n]) + (u[:, n:] + dot(high, last)))
 
 
@@ -825,18 +826,14 @@
     solve(place, buffers[0], semaphores(0), main, factor, first, pending, fill)
     source(first, src)
     to_modes(src, buffers[1][0])
-    fill = (
-        lambda: keep_curvatures(first, kept, range(8)),
-        lambda: weigh_counts(bias, counts, weighted),
-        None,
-        lambda: keep_curvatures(first, kept, range(8, 16)),
-    )
-    solve(place, buffers[1], semaphores(1), main, factor, second, pending, fill)
+    solve(place, buffers[1], semaphores(1), main, factor, second, pending)
     hand = Handover(row, col, payload, arrived, [hand_sem.at[i] for i in range(3)])
     paint(first, second, to_slot, ax, ay, az, spread, payload, total, fracs, tz, tt, hand)
+    weigh_counts(bias, counts, weighted)
     hand.arrive(pending)
     hand = Handover(row, col, back, returned, [hand_sem.at[i] for i in range(3, 6)])
     own_cells(nbar, bias, arrived, weighted, density, back, dens, pulls, hand)
+    keep_curvatures(first, kept, range(NZ))
     hand.arrive(pending)
     edges = []
     after = (

time: 134 us -> 134 us (level)
  no operation moved by 1% of the time
where the time goes in v7:
time: 134 us
  Pallas kernels  131 us (98%)
  local copies, waits for them, and re-layouts  2.26 us (2%)
    pallas_call x1, Pallas kernels, on_device(): pl.pallas_call(whole_kernel, out_shape=[jax.ShapeDtypeStruct((CX, CY * NZ...  131 us

profile of v7, /device:TPU:1, one launch (start us, length us, event | category | flops | bytes accessed | tf_op | source)
XLA Modules:
  0.0 133.7 jit_solution(12811600469852581172)
XLA Ops:
  0.6 130.8 %whole.1 = (f32[32,1024]{1,0:T(8,128)}, f32[32,1024]{1,0:T(8,128)}) custom-call(f32[8]{0:T(128)} %nbar.1, f32[8]{0:T(128)} %bias.1, f32[32,1024]{1,0:T(8,128)} %delta.1, s32[1,256]{1,0:T(1,128)} %bitcast.4, s32[1,256]{1,0:T(1,128)} %bitcast.5, s32[1,256]{1,0:T(1,128)} %bitcast.6, s32[1,256]{1,0:T(1,128)} %bitcast.7, s32[8,32,1024]{2,1,0:T(8,128)} %refs_0_.1, ...), custom_call_target="tpu_custom_call" | custom-call | tf_op jit(solution)/shard_map/whole/pallas_call | solution.py:906
  131.4 0.0 copy-start
  131.4 1.6 %copy.28 = f32[32,1024]{1,0:T(8,128)} copy(f32[32,1024]{1,0:T(8,128)} %get-tuple-element.4) | data formatting | bytes 262144
  133.0 0.0 copy-done
  133.0 0.7 copy.29
Async XLA Ops:
  131.4 1.6 %copy-start = (f32[32,1024]{1,0:T(8,128)S(1)}, f32[32,1024]{1,0:T(8,128)}, u32[]{:S(2)}) copy-start(f32[32,1024]{1,0:T(8,128)} %get-tuple-element.5) | copy-start | bytes 393220
